TPU v7x, 256 devices: a whole 4x4x8 slice. The times are simulated.
256 devices in a mesh: section: 8 (over z_hi, y), dp: 32 (over x, z_lo, core).
Axes of the slice: x: 4, y: 4, z: 8 (z_hi: 2, z_lo: 4; z = z_hi * 4 + z_lo), core: 2. Of those that a mesh axis runs over, the one named last changes fastest.
Arguments:
- layer_input: bfloat16 [8, 4096, 4, 128], P('section', 'dp'), may hold values from 0 to 1
- gate_weight: bfloat16 [8, 4096, 16384], P('section', None, 'dp'), may hold values from -0.09375 to 0.09375
- up_weight: bfloat16 [8, 4096, 16384], P('section', None, 'dp'), may hold values from -0.09375 to 0.09375
- down_weight: bfloat16 [8, 16384, 4096], P('section', 'dp'), may hold values from -0.046875 to 0.046875
- hidden_threshold: int32 [8, 16384], P('section', 'dp'), may hold values from 1 to 5
- hidden_width: int32 [8, 16384], P('section', 'dp'), may hold values from 1 to 5
- out_threshold: int32 [8, 4096], P('section', 'dp'), may hold values from 1 to 5
- out_width: int32 [8, 4096], P('section', 'dp'), may hold values from 1 to 5
- out_cotangent: bfloat16 [8, 4096, 4, 128], P('section', 'dp'), may hold values from -6 to 6
Outputs:
- incoming_spikes: bfloat16 [8, 4096, 4, 128], P('section', 'dp')
- returned_grads: bfloat16 [8, 4096, 4, 128], P('section', 'dp')
All inputs are finite; a program needn't handle non-finite values.
Results may differ from a plain program's by a relative error of at most 0.013.
Values may be sent and summed in bfloat16 or wider, within the bound.
A program may use at most 128 MiB of HBM per device.

v0:
```python
import jax
import jax.numpy as jnp
from jax import lax
from jax.sharding import PartitionSpec as P

T_STEPS = 4


decay_rate = 0.9
level_unit = 0.125


def with_halo(block, sides, width):
    for axis, dim in sides:
        count = lax.axis_size(axis)
        forward = [(i, i + 1) for i in range(count - 1)]
        backward = [(target, source) for source, target in forward]
        low = lax.ppermute(
            lax.slice_in_dim(block, block.shape[dim] - width, None, axis=dim), axis, forward
        )
        high = lax.ppermute(lax.slice_in_dim(block, 0, width, axis=dim), axis, backward)
        block = jnp.concatenate([low, block, high], axis=dim)
    return block


def soft_spikes(currents, threshold_level, width_level):
    threshold = level_unit * threshold_level.astype(currents[0].dtype)
    width = level_unit * width_level.astype(currents[0].dtype)
    potential = jnp.zeros_like(currents[0])
    spikes = jnp.zeros_like(currents[0])
    emitted = []
    for current in currents:
        potential = decay_rate * (potential - threshold * spikes) + current
        spikes = jax.nn.sigmoid((potential - threshold) / width)
        emitted.append(spikes)
    return emitted


def split_steps(matrix, count, axis):
    return [lax.slice_in_dim(matrix, k * count, (k + 1) * count, axis=axis) for k in range(T_STEPS)]


def contract(left, right, left_dim, right_dim):
    return lax.dot_general(
        left, right, (((left_dim,), (right_dim,)), ((), ())), preferred_element_type=jnp.float32
    )


def per_device(
    layer_input,
    gate_weight,
    up_weight,
    down_weight,
    hidden_threshold,
    hidden_width,
    out_threshold,
    out_width,
    out_cotangent,
):
    local_rows = layer_input.shape[1]
    steps_count = layer_input.shape[2]
    tokens = layer_input.shape[3]
    rows = steps_count * tokens
    gate_w = gate_weight[0]
    up_w = up_weight[0]
    down_w = down_weight[0]

    def hidden_fn(gate_in, up_in):
        return soft_spikes(
            split_steps(jax.nn.silu(gate_in) * up_in, tokens, 0),
            hidden_threshold[0],
            hidden_width[0],
        )

    piece = lax.all_gather(layer_input, "dp", axis=1, tiled=True)
    count = piece.shape[1]
    flat = piece.reshape(count, rows)
    gate_part = gate_w
    up_part = up_w
    gate = contract(flat, gate_part, 0, 0)
    upward = contract(flat, up_part, 0, 0)
    hidden_list, hidden_back = jax.vjp(hidden_fn, gate, upward)
    spikes = jnp.concatenate(hidden_list, 0).astype(jnp.bfloat16)
    part = down_w
    projected = lax.psum_scatter(
        contract(part, spikes, 0, 1), "dp", scatter_dimension=0, tiled=True
    )
    current = projected + layer_input[0].reshape(local_rows, rows).astype(jnp.float32)
    level_own = out_threshold[0][:, None]
    spread_own = out_width[0][:, None]

    def out_fn(total):
        return soft_spikes(split_steps(total, tokens, 1), level_own, spread_own)

    out_list, out_back = jax.vjp(out_fn, current)
    emitted = jnp.concatenate(out_list, 1).astype(jnp.bfloat16)
    cotangent = out_cotangent[0].reshape(local_rows, rows).astype(jnp.float32)
    current_grad = out_back(split_steps(cotangent, tokens, 1))[0]
    grad_block = current_grad.astype(jnp.bfloat16).reshape(1, local_rows, steps_count, tokens)
    piece = lax.all_gather(grad_block, "dp", axis=1, tiled=True)
    count = piece.shape[1]
    flat = piece.reshape(count, rows)
    part = down_w
    spike_grad = contract(flat, part, 0, 1)
    emitted_block = emitted.reshape(1, local_rows, steps_count, tokens)
    gate_grad, up_grad = hidden_back(split_steps(spike_grad, tokens, 0))
    gate_grad = gate_grad.astype(jnp.bfloat16)
    up_grad = up_grad.astype(jnp.bfloat16)
    gate_part = gate_w
    up_part = up_w
    summed = lax.psum_scatter(
        (contract(gate_part, gate_grad, 1, 1) + contract(up_part, up_grad, 1, 1)).astype(
            jnp.bfloat16
        ),
        "dp",
        scatter_dimension=0,
        tiled=True,
    ).astype(jnp.float32)
    input_grad = (
        (summed + current_grad).astype(jnp.bfloat16).reshape(1, local_rows, steps_count, tokens)
    )
    stacked = jnp.concatenate([input_grad, emitted_block], 0)
    extended = with_halo(stacked, (("section", 0),), 1)
    incoming = extended[0:1]
    returned = extended[3:4]
    return (incoming, returned)


def solution(mesh):
    placed = (
        P("section", "dp", None, None),
        P("section", None, "dp"),
        P("section", None, "dp"),
        P("section", "dp", None),
        P("section", "dp"),
        P("section", "dp"),
        P("section", "dp"),
        P("section", "dp"),
        P("section", "dp", None, None),
    )
    return jax.shard_map(
        per_device,
        mesh=mesh,
        in_specs=placed,
        out_specs=(P("section", "dp", None, None), P("section", "dp", None, None)),
        check_vma=False,
    )
```

profile of v0, /device:TPU:24, one launch (start us, length us, event | category | flops | bytes accessed | tf_op | source)
XLA Modules:
  0.0 516.9 jit_solution(5112177774291144709)
XLA Ops:
  7.2 0.0 all-gather.3.cloned.1.call-start
  7.2 0.7 all-gather.3.cloned.1.call-update
  7.9 0.0 reduce-scatter.5.cloned.1.call-start
  7.9 0.7 convert_multiply_fusion.1
  8.6 0.7 convert_multiply_fusion
  9.3 66.2 %all-gather.3.cloned.1.call-done = bf16[1,4096,4,128]{3,2,0,1:T(4,128)(2,1)} async-done(((bf16[1,128,4,128]{3,2,0,1:T(4,128)(2,1)}), bf16[1,4096,4,128]{3,2,0,1:T(4,128)(2,1)}) %all-gather.3.cloned.1.call-update) | async-done | bytes 4194320 | tf_op jit(solution)/shard_map/all_gather | solution.py:75
  75.5 6.0 %fusion.3 = f32[512,512]{1,0:T(8,128)S(1)} fusion(bf16[1,4096,512]{2,1,0:T(8,128)(2,1)} %param.10, bf16[512,8,4,128]{3,2,1,0:T(4,128)(2,1)} %bitcast.63), kind=kOutput, calls=%fused_computation.5 | convolution fusion | flops 2147483648 | bytes 9437184 | tf_op jit(solution)/shard_map/dot_general | solution.py:44
  81.5 0.0 copy-done.1
  81.5 0.0 copy-start
  81.5 3.4 fusion.46
  84.9 0.2 fusion.73
  85.1 0.2 fusion.81
  85.3 0.2 fusion.82
  85.5 5.6 %convolution_bitcast_fusion = f32[4096,512]{0,1:T(8,128)} fusion(bf16[1,512,4096]{2,1,0:T(8,128)(2,1)S(1)} %copy-done, bf16[128,512]{1,0:T(8,128)(2,1)S(1)} %get-tuple-element.17, bf16[128,512]{1,0:T(8,128)(2,1)S(1)} %get-tuple-element.15, bf16[128,512]{1,0:T(8,128)(2,1)S(1)} %get-tuple-element.13, bf16[128,512]{1,0:T(8,128)(2,1)S(1)} %get-tuple-element.19), kind=kOutput, calls=%fused_computation.1 | convolution fusion | flops 2149580800 | bytes 13107200 | tf_op jit(solution)/shard_map/dot_general | solution.py:44
  91.2 0.0 reduce-scatter.5.cloned.1.call-update
  91.2 0.0 all-gather.5.cloned.1.call-start
  91.2 0.8 copy-done.3
  92.1 0.1 copy.16
  92.2 0.0 copy-done.4
  92.2 0.1 copy.18
  92.3 1.2 multiply_bitcast_fusion.2
  93.5 158.9 %reduce-scatter.5.cloned.1.call-done = f32[128,512]{0,1:T(8,128)} async-done(((f32[4096,512]{0,1:T(8,128)}), f32[128,512]{0,1:T(8,128)}) %reduce-scatter.5.cloned.1.call-update) | async-done | bytes 262160 | tf_op jit(solution)/shard_map/reduce_scatter | solution.py:85
  252.4 1.0 bitcast_add_fusion
  253.4 1.4 fusion.58
  254.8 0.7 fusion.47
  255.5 0.0 all-gather.5.cloned.1.call-update
  255.5 0.2 reduce-scatter.7.cloned.1.call-start
  255.7 66.9 %all-gather.5.cloned.1.call-done = bf16[1,4096,4,128]{1,3,2,0:T(8,128)(2,1)} async-done(((bf16[1,128,4,128]{1,3,2,0:T(8,128)(2,1)}), bf16[1,4096,4,128]{1,3,2,0:T(8,128)(2,1)}) %all-gather.5.cloned.1.call-update) | async-done | bytes 4194320 | tf_op jit(solution)/shard_map/all_gather | solution.py:100
  322.7 6.0 %fusion.5 = f32[512,512]{1,0:T(8,128)S(1)} fusion(bf16[4096,512]{0,1:T(8,128)(2,1)} %bitcast.65, bf16[1,512,4096]{2,1,0:T(8,128)(2,1)} %param.12), kind=kOutput, calls=%fused_computation.7 | convolution fusion | flops 2147483648 | bytes 9437184 | tf_op jit(solution)/shard_map/dot_general | solution.py:44
  328.7 0.4 fusion.38
  329.1 0.0 copy-done.7
  329.1 0.0 copy-start.2
  329.1 2.5 fusion.10
  331.6 4.4 fusion
  336.1 6.5 %copy.20 = bf16[4096,512]{1,0:T(8,128)(2,1)} copy(bf16[4096,512]{0,1:T(8,128)(2,1)} %fusion) | data formatting | bytes 8388608
  342.5 0.0 reduce-scatter.7.cloned.1.call-update
  342.5 0.6 copy-done.6
  343.2 0.1 copy-done.5
  343.3 0.1 copy.17
  343.4 6.4 %collective-permute-start = (bf16[1,128,4,128]{3,2,1,0:T(4,128)(2,1)S(1)}, bf16[1,128,4,128]{3,2,1,0:T(4,128)(2,1)S(1)}, u32[]{:S(2)}, u32[]{:S(2)}) collective-permute-start(bf16[1,128,4,128]{3,2,1,0:T(4,128)(2,1)S(1)} %copy.17), channel_id=1, source_target_pairs={{0,32},{32,64},{64,96},{96,128},{128,160},{160,192},{192,224},{1,3... | collective-permute-start | bytes 393224 | tf_op jit(solution)/shard_map/ppermute | solution.py:18
  349.9 145.1 %reduce-scatter.7.cloned.1.call-done = bf16[128,512]{1,0:T(8,128)(2,1)} async-done(((bf16[4096,512]{1,0:T(8,128)(2,1)}), bf16[128,512]{1,0:T(8,128)(2,1)}) %reduce-scatter.7.cloned.1.call-update) | async-done | bytes 131088
  495.0 1.0 copy.21
  496.0 0.1 copy.19
  496.2 2.7 collective-permute-start.1
  498.9 0.0 collective-permute-done
  498.9 10.2 %collective-permute-done.1 = bf16[1,128,4,128]{3,2,1,0:T(4,128)(2,1)S(1)} collective-permute-done((bf16[1,128,4,128]{3,2,1,0:T(4,128)(2,1)S(1)}, bf16[1,128,4,128]{3,2,1,0:T(4,128)(2,1)S(1)}, u32[]{:S(2)}, u32[]{:S(2)}) %collective-permute-start.1) | collective-permute-done | bytes 131104 | tf_op jit(solution)/shard_map/ppermute | solution.py:21
  509.1 0.7 copy.35
  509.7 0.7 copy.36
  (16 shorter events, 0.1 us)
Async XLA Ops:
  7.2 68.3 %all-gather.3.cloned.1.call-start = ((), (), s32[]{:S(2)}) async-start(), calls=%async_computation.2 | async-start | bytes 4325376 | tf_op jit(solution)/shard_map/all_gather | solution.py:75
  7.9 244.5 %reduce-scatter.5.cloned.1.call-start = ((), (), s32[]{:S(2)}) async-start(), calls=%async_computation.3 | async-start | bytes 8650752 | tf_op jit(solution)/shard_map/reduce_scatter | solution.py:85
  75.5 6.0 %copy-start.1 = (bf16[1,4096,512]{2,1,0:T(8,128)(2,1)S(1)}, bf16[1,4096,512]{2,1,0:T(8,128)(2,1)}, u32[]{:S(2)}) copy-start(bf16[1,4096,512]{2,1,0:T(8,128)(2,1)} %param.11) | copy-start | bytes 12582916
  75.5 6.0 %copy-start.8 = (bf16[1,4096,4,128]{3,2,0,1:T(4,128)(2,1)S(1)}, bf16[1,4096,4,128]{3,2,0,1:T(4,128)(2,1)}, u32[]{:S(2)}) copy-start(bf16[1,4096,4,128]{3,2,0,1:T(4,128)(2,1)} %all-gather.3.cloned.1.call-done) | copy-start | bytes 12582916
  81.5 4.1 copy-start
  91.2 0.9 copy-start.3
  91.2 1.0 copy-start.4
  91.2 231.5 %all-gather.5.cloned.1.call-start = ((), (), s32[]{:S(2)}) async-start(), calls=%async_computation.4 | async-start | bytes 4325376 | tf_op jit(solution)/shard_map/all_gather | solution.py:100
  255.5 239.5 %reduce-scatter.7.cloned.1.call-start = ((), (), s32[]{:S(2)}) async-start(), calls=%async_computation.5 | async-start | bytes 4325376
  322.7 6.4 %copy-start.7 = (bf16[1,4096,512]{2,1,0:T(8,128)(2,1)S(1)}, bf16[1,4096,512]{2,1,0:T(8,128)(2,1)}, u32[]{:S(2)}) copy-start(bf16[1,4096,512]{2,1,0:T(8,128)(2,1)} %param.10) | copy-start | bytes 12582916
  322.7 6.4 %copy-start.9 = (f32[512,512]{1,0:T(8,128)S(1)}, f32[512,512]{1,0:T(8,128)}, u32[]{:S(2)}) copy-start(f32[512,512]{1,0:T(8,128)} %get-tuple-element.24) | copy-start | bytes 3145732
  329.1 2.5 copy-start.2
  342.5 0.6 copy-start.6
  342.5 0.8 copy-start.5
  343.4 155.4 %collective-permute-start = (bf16[1,128,4,128]{3,2,1,0:T(4,128)(2,1)S(1)}, bf16[1,128,4,128]{3,2,1,0:T(4,128)(2,1)S(1)}, u32[]{:S(2)}, u32[]{:S(2)}) collective-permute-start(bf16[1,128,4,128]{3,2,1,0:T(4,128)(2,1)S(1)} %copy.17), channel_id=1, source_target_pairs={{0,32},{32,64},{64,96},{96,128},{128,160},{160,192},{192,224},{1,3... | collective-permute-start | bytes 393224 | tf_op jit(solution)/shard_map/ppermute | solution.py:18
  496.2 12.9 %collective-permute-start.1 = (bf16[1,128,4,128]{3,2,1,0:T(4,128)(2,1)S(1)}, bf16[1,128,4,128]{3,2,1,0:T(4,128)(2,1)S(1)}, u32[]{:S(2)}, u32[]{:S(2)}) collective-permute-start(bf16[1,128,4,128]{3,2,1,0:T(4,128)(2,1)S(1)} %copy.19), channel_id=1, source_target_pairs={{32,0},{64,32},{96,64},{128,96},{160,128},{192,160},{224,192},{33,... | collective-permute-start | bytes 393224 | tf_op jit(solution)/shard_map/ppermute | solution.py:21
Sparse Core Ops, SparseCore 0:
  9.9 65.6 all-gather.2
  91.3 161.0 reduce-scatter.4
  255.6 67.0 all-gather.4
  342.7 152.2 reduce-scatter.6
where the time goes:
time: 517 us
  waiting for transfers between devices  448 us (87%)
  matrix products  27.9 us (5%)
  between operations  14 us (3%)
  local copies, waits for them, and re-layouts  10.9 us (2%)
  starting transfers between devices  9.46 us (2%)
  other arithmetic  6.69 us (1%)
    reduce_scatter x1, waiting for transfers between devices, per_device(): lax.psum_scatter(contract(part, spikes, 0, 1), 'dp', scatter_dimension=0,...  159 us
    unnamed x5, waiting for transfers between devices  146 us
    all_gather x1, waiting for transfers between devices, per_device(): piece = lax.all_gather(grad_block, 'dp', axis=1, tiled=True)  66.9 us
    all_gather x1, waiting for transfers between devices, per_device(): piece = lax.all_gather(layer_input, 'dp', axis=1, tiled=True)  66.2 us
    dot_general x6, matrix products, contract(): lax.dot_general(left, right, (((left_dim,), (right_dim,)), ((), ())), pre...  27.9 us
  transfers between devices with their start and end apart: 6, of which 5 were waited for; matrix products, arithmetic and copies ran while one was open for 1% of the time, Pallas kernels for 0%

commit v1 on v0

v1 whole, which is shorter than its diff:
```python
import functools

import jax
import jax.numpy as jnp
from jax import lax
from jax.experimental import pallas as pl
from jax.experimental.pallas import tpu as pltpu
from jax.sharding import PartitionSpec as P

MESH = pl.DeviceIdType.MESH
F32, BF16 = jnp.float32, jnp.bfloat16
DECAY, UNIT = 0.9, 0.125
STEPS = 4
NX, NZ = 4, 4
TOK = 128
ROWS = STEPS * TOK
BLK = 128
HID = 512
HALF = ROWS // 2


def sigmoid(v):
    return 1.0 / (1.0 + jnp.exp(-v))


def kernel(
    x_ref, cot_ref, hth_ref, hwd_ref, oth_ref, owd_ref, gate_hbm, up_hbm, down_hbm,
    inc_ref, ret_ref,
    wg, wu, dw, xg, cg, gate, up, spk, hs, sg, gg, ug, own, cgf,
    acc, sib_send, opp_send, rl_send, z_send,
    sib_recv, opp_recv, rl_recv, z_recv, em_send, ig_send,
    w_sem, d_sem, ag_ss, ag_rm, ag_rh, ag_rs, rs_ss, rs_sib, rs_opp, rs_rl, rs_z, sec_s, sec_r,
):
    me = lax.axis_index("dp")
    sec = lax.axis_index("section")
    n_sec = lax.axis_size("section")
    c = me % 2
    z = (me // 2) % NZ
    x = me // (2 * NZ)

    def dev(xx, zz, cc):
        return {"dp": (xx * NZ + zz) * 2 + cc}

    xp, xm, xo = (x + 1) % NX, (x + 3) % NX, (x + 2) % NX
    to_sib, to_xp, to_xm = dev(x, z, 1 - c), dev(xp, z, c), dev(xm, z, c)
    to_zp, to_zm = dev(x, (z + 1) % NZ, c), dev(x, (z + 3) % NZ, c)
    to_next, to_prev = {"section": (sec + 1) % n_sec}, {"section": (sec + n_sec - 1) % n_sec}

    def zorder(k):
        m = z // 2
        near = m * (3 - z) + (1 - m) * z
        low = 1 - k // 2
        o = low * (k * (1 - near) + (1 - k) * near) + (1 - low) * k
        return m * (3 - o) + (1 - m) * o

    def weight_copies():
        gu, dn = [], []
        for zz in range(NZ):
            for r in range(2):
                cc = c if r == 0 else 1 - c
                for i, (src, dst) in enumerate(((gate_hbm, wg), (up_hbm, wu))):
                    gu.append(pltpu.make_async_copy(src.at[:, zz, cc], dst.at[zz, r], w_sem.at[i, zz, r]))
                for xx in range(NX):
                    col = pl.multiple_of(((xx * NZ + zz) * 2 + cc) * BLK, BLK)
                    dn.append(
                        pltpu.make_async_copy(
                            down_hbm.at[:, pl.ds(col, BLK)],
                            dw.at[zz, r, :, pl.ds(xx * BLK, BLK)],
                            d_sem.at[zz, r, xx],
                        )
                    )
        return gu, dn

    gu_copies, dn_copies = weight_copies()
    for cp in gu_copies + dn_copies:
        cp.start()
    xg[z, 0, x] = x_ref[...]

    bar = pltpu.get_barrier_semaphore()

    def greet(d):
        pl.semaphore_signal(bar, inc=1, device_id=d, device_id_type=MESH)

    for d in (to_sib, to_xp, to_xm):
        greet(d)
    for cond, d in ((z > 0, to_zm), (z < NZ - 1, to_zp), (sec > 0, to_prev), (sec < n_sec - 1, to_next)):
        pl.when(cond)(functools.partial(greet, d))
    peers = 3
    for cond in (z > 0, z < NZ - 1, sec > 0, sec < n_sec - 1):
        peers = peers + cond.astype(jnp.int32)
    pl.semaphore_wait(bar, peers)

    def remote(src, dst, ss, rs, d):
        return pltpu.make_async_remote_copy(
            src_ref=src, dst_ref=dst, send_sem=ss, recv_sem=rs, device_id=d, device_id_type=MESH
        )

    class Gather:
        def __init__(self, n, buf):
            self.n, self.buf = n, buf

        def whole(self, kind, k, zz, xx, d):
            ref = self.buf.at[zz, 0, xx]
            return remote(ref, ref, ag_ss.at[self.n, kind, k], ag_rm.at[self.n, zz, xx], d)

        def half(self, kind, k, zz, xx, h, d):
            ref = self.buf.at[zz, 0, xx, pl.ds(h * HALF, HALF)]
            return remote(ref, ref, ag_ss.at[self.n, kind, k], ag_rh.at[self.n, zz, h], d)

        def sib(self, kind, k, zz, xx):
            return remote(
                self.buf.at[zz, 0, xx], self.buf.at[zz, 1, xx],
                ag_ss.at[self.n, kind, k], ag_rs.at[self.n, zz, xx], to_sib,
            )

        def z_stage(self, k):
            zz = zorder(k)
            pl.when(k > 0)(lambda: self.whole(0, k, zz, x, to_zp).wait_recv())
            self.whole(2, k, zz, x, to_xp).start()
            self.whole(3, k, zz, x, to_xm).start()
            pl.when((zz <= z) & (z < NZ - 1))(lambda: self.whole(0, k, zz, x, to_zp).start())
            pl.when((zz >= z) & (z > 0))(lambda: self.whole(1, k, zz, x, to_zm).start())
            self.sib(4, k, zz, x).start()

        def x_stage(self, k):
            zz = zorder(k)
            self.whole(2, k, zz, xm, to_xp).wait_recv()
            self.half(5, k, zz, xm, 0, to_xp).start()
            self.whole(3, k, zz, xp, to_xm).wait_recv()
            self.half(7, k, zz, xp, 1, to_xm).start()
            self.sib(6, k, zz, xm).start()
            self.sib(8, k, zz, xp).start()

        def last_stage(self, k):
            zz = zorder(k)
            self.half(5, k, zz, xo, 0, to_xp).wait_recv()
            self.half(7, k, zz, xo, 1, to_xm).wait_recv()
            self.sib(9, k, zz, xo).start()
            for xx in range(NX):
                self.sib(9, k, zz, xx).wait_recv()

        def drain(self):
            @pl.loop(0, NZ)
            def _(k):
                zz = zorder(k)
                pl.when((zz <= z) & (z < NZ - 1))(lambda: self.whole(0, k, zz, x, to_zp).wait_send())
                pl.when((zz >= z) & (z > 0))(lambda: self.whole(1, k, zz, x, to_zm).wait_send())
                self.whole(2, k, zz, x, to_xp).wait_send()
                self.whole(3, k, zz, x, to_xm).wait_send()
                self.half(5, k, zz, xm, 0, to_xp).wait_send()
                self.half(7, k, zz, xp, 1, to_xm).wait_send()
                for kind, xx in ((4, x), (6, xm), (8, xp), (9, xo)):
                    self.sib(kind, k, zz, xx).wait_send()

        def run(self, compute):
            @pl.loop(0, NZ + 2)
            def _(s):
                pl.when(s < NZ)(lambda: self.z_stage(s))
                pl.when((s >= 1) & (s <= NZ))(lambda: self.x_stage(s - 1))

                @pl.when(s >= 2)
                def _():
                    self.last_stage(s - 2)
                    compute(zorder(s - 2))

    def gathered(buf, zz, r):
        return jnp.concatenate([buf[zz, r, xx] for xx in range(NX)], axis=1)

    class Scatter:
        def __init__(self, n):
            self.n = n

        def cols(self, xx):
            return pl.ds(pl.multiple_of(xx * BLK, BLK), BLK)

        def sib(self, k):
            return remote(
                sib_send.at[self.n, k], sib_recv.at[self.n, k],
                rs_ss.at[self.n, 0, k], rs_sib.at[self.n, k], to_sib,
            )

        def opp(self, k, h):
            return remote(
                opp_send.at[self.n, k, h], opp_recv.at[self.n, k, h],
                rs_ss.at[self.n, 1 + h, k], rs_opp.at[self.n, k, h], to_xp if h == 0 else to_xm,
            )

        def rl(self, k, h):
            return remote(
                rl_send.at[self.n, k, h], rl_recv.at[self.n, k, h],
                rs_ss.at[self.n, 3 + h, k], rs_rl.at[self.n, k, h], to_xp if h == 0 else to_xm,
            )

        def zz_copy(self, k, zz, h):
            return remote(
                z_send.at[self.n, k], z_recv.at[self.n, zz, h],
                rs_ss.at[self.n, 5, k], rs_z.at[self.n, zz, h], to_zp if h == 0 else to_zm,
            )

        def first(self, k, product):
            zz = zorder(3 - k)
            sib_send[self.n, k] = product(zz, 1).astype(BF16)
            self.sib(k).start()
            acc[k] = product(zz, 0)
            self.sib(k).wait_recv()
            for h in range(2):
                rows = pl.ds(h * HALF, HALF)
                opp_send[self.n, k, h] = (
                    acc[k, rows, self.cols(xo)] + sib_recv[self.n, k, rows, self.cols(xo)].astype(F32)
                ).astype(BF16)
                self.opp(k, h).start()

        def second(self, k):
            for h in range(2):
                xx = xp if h == 0 else xm
                with_opp, alone = pl.ds(h * HALF, HALF), pl.ds((1 - h) * HALF, HALF)
                rl_send[self.n, k, h, alone] = (
                    acc[k, alone, self.cols(xx)] + sib_recv[self.n, k, alone, self.cols(xx)].astype(F32)
                ).astype(BF16)
                part = acc[k, with_opp, self.cols(xx)] + sib_recv[self.n, k, with_opp, self.cols(xx)].astype(F32)
                self.opp(k, h).wait_recv()
                rl_send[self.n, k, h, with_opp] = (part + opp_recv[self.n, k, h].astype(F32)).astype(BF16)
                self.rl(k, h).start()

        def third(self, k):
            zz = zorder(3 - k)
            self.rl(k, 0).wait_recv()
            self.rl(k, 1).wait_recv()
            own[...] = (
                acc[k, :, self.cols(x)] + sib_recv[self.n, k, :, self.cols(x)].astype(F32)
                + (rl_recv[self.n, k, 0].astype(F32) + rl_recv[self.n, k, 1].astype(F32))
            )

            def add(h):
                self.zz_copy(k, zz, h).wait_recv()
                own[...] += z_recv[self.n, zz, h].astype(F32)

            def send(h):
                z_send[self.n, k] = own[...].astype(BF16)
                self.zz_copy(k, zz, h).start()

            pl.when((zz >= z) & (z > 0))(lambda: add(0))
            pl.when((zz <= z) & (z < NZ - 1))(lambda: add(1))
            pl.when(zz > z)(lambda: send(0))
            pl.when(zz < z)(lambda: send(1))

        def drain(self):
            @pl.loop(0, NZ)
            def _(k):
                zz = zorder(3 - k)
                self.sib(k).wait_send()
                for h in range(2):
                    self.opp(k, h).wait_send()
                    self.rl(k, h).wait_send()
                pl.when(zz > z)(lambda: self.zz_copy(k, zz, 0).wait_send())
                pl.when(zz < z)(lambda: self.zz_copy(k, zz, 1).wait_send())

        def run(self, product):
            @pl.loop(0, NZ + 2)
            def _(s):
                pl.when(s < NZ)(lambda: self.first(s, product))
                pl.when((s >= 1) & (s <= NZ))(lambda: self.second(s - 1))
                pl.when(s >= 2)(lambda: self.third(s - 2))

    first_gather, second_gather = Gather(0, xg), Gather(1, cg)
    gate[...] = jnp.zeros_like(gate)
    up[...] = jnp.zeros_like(up)
    for cp in gu_copies:
        cp.wait()

    def gate_up(zz):
        @pl.loop(0, 2)
        def _(r):
            lhs = gathered(xg, zz, r)
            gate[...] += jnp.dot(lhs, wg[zz, r].reshape(HID, HID), preferred_element_type=F32)
            up[...] += jnp.dot(lhs, wu[zz, r].reshape(HID, HID), preferred_element_type=F32)

    first_gather.run(gate_up)

    TILE = 32

    def tiles(body):
        @pl.loop(0, (HID // 128) * (TOK // TILE))
        def _(i):
            cols = pl.ds(pl.multiple_of((i // (TOK // TILE)) * 128, 128), 128)
            base = (i % (TOK // TILE)) * TILE
            body([pl.ds(pl.multiple_of(t * TOK + base, TILE), TILE) for t in range(STEPS)], cols)

    def hidden_forward(rows, cols):
        th = UNIT * hth_ref[:, cols].astype(F32)
        iw = 1.0 / (UNIT * hwd_ref[:, cols].astype(F32))
        p = jnp.zeros((TILE, 128), F32)
        s = jnp.zeros((TILE, 128), F32)
        for t in range(STEPS):
            g = gate[rows[t], cols]
            p = DECAY * (p - th * s) + g * sigmoid(g) * up[rows[t], cols]
            s = sigmoid((p - th) * iw)
            spk[rows[t], cols] = s
            hs[rows[t], cols] = s.astype(BF16)

    tiles(hidden_forward)

    for cp in dn_copies:
        cp.wait()
    first_scatter, second_scatter = Scatter(0), Scatter(1)
    first_scatter.run(lambda zz, r: jnp.dot(hs[...], dw[zz, r], preferred_element_type=F32))

    th = UNIT * oth_ref[...].astype(F32)
    iw = 1.0 / (UNIT * owd_ref[...].astype(F32))
    p = jnp.zeros((TOK, BLK), F32)
    s = jnp.zeros((TOK, BLK), F32)
    for t in range(STEPS):
        rows = pl.ds(t * TOK, TOK)
        p = DECAY * (p - th * s) + (own[rows] + x_ref[rows].astype(F32))
        s = sigmoid((p - th) * iw)
        own[rows] = s
        em_send[rows] = s.astype(BF16)
    dp = jnp.zeros((TOK, BLK), F32)
    for t in reversed(range(STEPS)):
        rows = pl.ds(t * TOK, TOK)
        s = own[rows]
        ds = cot_ref[rows].astype(F32) - (DECAY * th) * dp
        dp = DECAY * dp + ds * (s * (1.0 - s) * iw)
        cgf[rows] = dp
        cg[z, 0, x, rows] = dp.astype(BF16)

    emit = remote(em_send, inc_ref, sec_s.at[0], sec_r.at[0], to_next)
    back = remote(ig_send, ret_ref, sec_s.at[1], sec_r.at[1], to_prev)
    pl.when(sec < n_sec - 1)(emit.start)

    sg[...] = jnp.zeros_like(sg)

    def spike_grad(zz):
        @pl.loop(0, 2)
        def _(r):
            sg[...] += lax.dot_general(
                gathered(cg, zz, r), dw[zz, r], (((1,), (1,)), ((), ())), preferred_element_type=F32
            )

    second_gather.run(spike_grad)

    def hidden_backward(rows, cols):
        th = UNIT * hth_ref[:, cols].astype(F32)
        iw = 1.0 / (UNIT * hwd_ref[:, cols].astype(F32))
        dp = jnp.zeros((TILE, 128), F32)
        for t in reversed(range(STEPS)):
            s = spk[rows[t], cols]
            ds = sg[rows[t], cols] - (DECAY * th) * dp
            dp = DECAY * dp + ds * (s * (1.0 - s) * iw)
            g = gate[rows[t], cols]
            q = sigmoid(g)
            ug[rows[t], cols] = (dp * (g * q)).astype(BF16)
            gg[rows[t], cols] = (dp * up[rows[t], cols] * (q * (1.0 + g * (1.0 - q)))).astype(BF16)

    tiles(hidden_backward)

    def input_grad(zz, r):
        nt = (((1,), (1,)), ((), ()))
        return lax.dot_general(
            gg[...], wg[zz, r].reshape(HID, HID), nt, preferred_element_type=F32
        ) + lax.dot_general(ug[...], wu[zz, r].reshape(HID, HID), nt, preferred_element_type=F32)

    second_scatter.run(input_grad)
    ig_send[...] = (own[...] + cgf[...]).astype(BF16)

    pl.when(sec > 0)(back.start)

    def clear(ref):
        ref[...] = jnp.zeros_like(ref)

    pl.when(sec == 0)(lambda: clear(inc_ref))
    pl.when(sec == n_sec - 1)(lambda: clear(ret_ref))
    for phase in (first_gather, first_scatter, second_gather, second_scatter):
        phase.drain()
    pl.when(sec < n_sec - 1)(emit.wait_send)
    pl.when(sec > 0)(emit.wait_recv)
    pl.when(sec > 0)(back.wait_send)
    pl.when(sec < n_sec - 1)(back.wait_recv)


def per_device(layer_input, gate_w, up_w, down_w, hth, hwd, oth, owd, cotangent):
    def turned(a):
        return a[0].transpose(1, 2, 0).reshape(ROWS, BLK)

    vmem, hbm, dma = pltpu.VMEM, pl.BlockSpec(memory_space=pl.ANY), pltpu.SemaphoreType.DMA
    local = pl.BlockSpec(memory_space=pltpu.VMEM)
    blocked = (NX, NZ, 2, BLK, HID)
    incoming, returned = pl.pallas_call(
        kernel,
        out_shape=(jax.ShapeDtypeStruct((ROWS, BLK), BF16),) * 2,
        in_specs=[local] * 6 + [hbm] * 3,
        out_specs=(local, local),
        scratch_shapes=[
            vmem((NZ, 2, NX, BLK, HID), BF16),
            vmem((NZ, 2, NX, BLK, HID), BF16),
            vmem((NZ, 2, HID, NX * BLK), BF16),
            vmem((NZ, 2, NX, ROWS, BLK), BF16),
            vmem((NZ, 2, NX, ROWS, BLK), BF16),
            vmem((ROWS, HID), F32),
            vmem((ROWS, HID), F32),
            vmem((ROWS, HID), F32),
            vmem((ROWS, HID), BF16),
            vmem((ROWS, HID), F32),
            vmem((ROWS, HID), BF16),
            vmem((ROWS, HID), BF16),
            vmem((ROWS, BLK), F32),
            vmem((ROWS, BLK), F32),
            vmem((NZ, ROWS, NX * BLK), F32),
            vmem((2, NZ, ROWS, NX * BLK), BF16),
            vmem((2, NZ, 2, HALF, BLK), BF16),
            vmem((2, NZ, 2, ROWS, BLK), BF16),
            vmem((2, NZ, ROWS, BLK), BF16),
            vmem((2, NZ, ROWS, NX * BLK), BF16),
            vmem((2, NZ, 2, HALF, BLK), BF16),
            vmem((2, NZ, 2, ROWS, BLK), BF16),
            vmem((2, NZ, 2, ROWS, BLK), BF16),
            vmem((ROWS, BLK), BF16),
            vmem((ROWS, BLK), BF16),
            dma((2, NZ, 2)),
            dma((NZ, 2, NX)),
            dma((2, 10, NZ)),
            dma((2, NZ, NX)),
            dma((2, NZ, 2)),
            dma((2, NZ, NX)),
            dma((2, 6, NZ)),
            dma((2, NZ)),
            dma((2, NZ, 2)),
            dma((2, NZ, 2)),
            dma((2, NZ, 2)),
            dma((2,)),
            dma((2,)),
        ],
        compiler_params=pltpu.CompilerParams(
            collective_id=0, has_side_effects=True, vmem_limit_bytes=60 * 2**20
        ),
        cost_estimate=pl.CostEstimate(
            flops=12 * ROWS * HID * 4096, bytes_accessed=12 * 2**20, transcendentals=2**20
        ),
        name="layer",
    )(
        turned(layer_input), turned(cotangent), hth, hwd, oth, owd,
        gate_w.reshape(blocked), up_w.reshape(blocked), down_w.reshape(HID, -1),
    )

    def restored(a):
        return a.reshape(STEPS, TOK, BLK).transpose(2, 0, 1)[None]

    return restored(incoming), restored(returned)


def solution(mesh):
    placed = (
        P("section", "dp", None, None),
        P("section", None, "dp"),
        P("section", None, "dp"),
        P("section", "dp", None),
        P("section", "dp"),
        P("section", "dp"),
        P("section", "dp"),
        P("section", "dp"),
        P("section", "dp", None, None),
    )
    return jax.shard_map(
        per_device,
        mesh=mesh,
        in_specs=placed,
        out_specs=(P("section", "dp", None, None), P("section", "dp", None, None)),
        check_vma=False,
    )
```

time: 517 us -> 150 us (0.29)
  waiting for transfers between devices: 448 us -> 0 us
  Pallas kernels: 0 us -> 142 us
  matrix products: 27.9 us -> 0 us
  between operations: 14 us -> 0.64 us
  starting transfers between devices: 9.46 us -> 0 us
  other arithmetic: 6.69 us -> 0 us
    reduce_scatter x1 -> x0, waiting for transfers between devices: 159 us -> none  [per_device(): lax.psum_scatter(contract(part, spikes, 0, 1), 'dp', scatter_dimension=0,...]
    unnamed x5 -> x0, waiting for transfers between devices: 146 us -> none
    pallas_call x0 -> x1, Pallas kernels: none -> 142 us  [per_device(): pl.pallas_call(kernel, out_shape=(jax.ShapeDtypeStruct((ROWS, BLK), BF16)...]
    all_gather x2 -> x0, waiting for transfers between devices: 133 us -> none  [the longest x1 66.9 us: per_device(): piece = lax.all_gather(grad_block, 'dp', axis=1, tiled=True)]
    dot_general x6 -> x0, matrix products: 27.9 us -> none  [contract(): lax.dot_general(left, right, (((left_dim,), (right_dim,)), ((), ())), pre...]
    unnamed x24 -> x0, local copies, waits for them, and re-layouts: 10.3 us -> none
    ppermute x2 -> x0, waiting for transfers between devices: 10.2 us -> none  [the longest x1 10.2 us: with_halo(): lax.ppermute(lax.slice_in_dim(block, 0, width, axis=dim), axis, backward)]
    ppermute x2 -> x0, starting transfers between devices: 9.12 us -> none  [the longest x1 6.45 us: with_halo(): lax.ppermute(lax.slice_in_dim(block, block.shape[dim] - width, None, axis...]
  transfers between devices with their start and end apart: 6 -> 0, of which waited for: 5 -> 0; matrix products, arithmetic and copies ran while one was open for 1% -> 0% of each run, Pallas kernels for 0% -> 0%
where the time goes in v1:
time: 150 us; the launch traced here: 149 us
  Pallas kernels  142 us (95%)
  local copies, waits for them, and re-layouts  6.71 us (4%)
    pallas_call x1, Pallas kernels, per_device(): pl.pallas_call(kernel, out_shape=(jax.ShapeDtypeStruct((ROWS, BLK), BF16)...  142 us
    reshape x2, local copies, waits for them, and re-layouts, restored(): return a.reshape(STEPS, TOK, BLK).transpose(2, 0, 1)[None]  3.37 us
    transpose x2, local copies, waits for them, and re-layouts, turned(): return a[0].transpose(1, 2, 0).reshape(ROWS, BLK)  3.34 us

profile of v1, /device:TPU:24, one launch (start us, length us, event | category | flops | bytes accessed | tf_op | source)
XLA Modules:
  0.0 149.3 jit_solution(10405956750118382137)
XLA Ops:
  0.6 1.7 %copy.11 = bf16[4,128,128]{2,1,0:T(8,128)(2,1)} copy(bf16[4,128,128]{1,0,2:T(4,128)(2,1)} %bitcast.19) | data formatting | bytes 262144 | tf_op jit(solution)/shard_map/transpose | solution.py:383
  2.3 1.7 %copy.12 = bf16[4,128,128]{2,1,0:T(8,128)(2,1)} copy(bf16[4,128,128]{1,0,2:T(4,128)(2,1)} %bitcast.20) | data formatting | bytes 262144 | tf_op jit(solution)/shard_map/transpose | solution.py:383
  4.0 141.9 %layer.1 = (bf16[512,128]{1,0:T(8,128)(2,1)}, bf16[512,128]{1,0:T(8,128)(2,1)}) custom-call(bf16[512,128]{1,0:T(8,128)(2,1)} %bitcast.25, bf16[512,128]{1,0:T(8,128)(2,1)} %bitcast.26, s32[1,512]{1,0:T(1,128)} %hth_ref.1, s32[1,512]{1,0:T(1,128)} %hwd_ref.1, s32[1,128]{1,0:T(1,128)} %oth_ref.1, s32[1,128]{1,0:T(1,128)} %owd_ref.1, ...), custom_call_target="tpu_custom_call" | custom-call | flops 12884901888 | bytes 12582912 | tf_op jit(solution)/shard_map/layer/pallas_call | solution.py:388
  145.9 1.7 %copy.13 = bf16[4,128,128]{1,0,2:T(4,128)(2,1)} copy(bf16[4,128,128]{2,1,0:T(8,128)(2,1)} %bitcast.24) | data formatting | bytes 262144 | tf_op jit(solution)/shard_map/reshape | solution.py:446
  147.6 1.7 %copy.14 = bf16[4,128,128]{1,0,2:T(4,128)(2,1)} copy(bf16[4,128,128]{2,1,0:T(8,128)(2,1)} %bitcast.23) | data formatting | bytes 262144 | tf_op jit(solution)/shard_map/reshape | solution.py:446

commit v2 on v0

v2 whole, which is shorter than its diff:
```python
import functools

import jax
import jax.numpy as jnp
from jax import lax
from jax.experimental import pallas as pl
from jax.experimental.pallas import tpu as pltpu
from jax.sharding import PartitionSpec as P

MESH = pl.DeviceIdType.MESH
F32, BF16 = jnp.float32, jnp.bfloat16
DECAY, UNIT = 0.9, 0.125
STEPS = 4
NX, NZ = 4, 4
TOK = 128
ROWS = STEPS * TOK
BLK = 128
HID = 512
STREAMS = 2
STOK = TOK // STREAMS
SROWS = STEPS * STOK
HALF = SROWS // 2
G = STREAMS * NZ


def sigmoid(v):
    return 0.5 + 0.5 * jnp.tanh(0.5 * v)


def kernel(
    x_ref, cot_ref, hth_ref, hwd_ref, oth_ref, owd_ref, gate_hbm, up_hbm, down_hbm,
    inc_ref, ret_ref,
    wg, wu, dw, xg, cg, gate, up, spk, hs, sg, gg, ug, tz, cgf,
    cot, acc, sib_send, opp_send, rl_send, z_send,
    sib_recv, opp_recv, rl_recv, z_recv, em_send, ig_send, em_recv, ig_recv,
    w_sem, d_sem, ag_ss, ag_rm, ag_rh, ag_rs, rs_ss, rs_sib, rs_opp, rs_rl, rs_z, sec_s, sec_r,
):
    me = lax.axis_index("dp")
    sec = lax.axis_index("section")
    n_sec = lax.axis_size("section")
    c = me % 2
    z = (me // 2) % NZ
    x = me // (2 * NZ)

    def dev(xx, zz, cc):
        return {"dp": (xx * NZ + zz) * 2 + cc}

    xp, xm, xo = (x + 1) % NX, (x + 3) % NX, (x + 2) % NX
    to_sib, to_xp, to_xm = dev(x, z, 1 - c), dev(xp, z, c), dev(xm, z, c)
    to_zp, to_zm = dev(x, (z + 1) % NZ, c), dev(x, (z + 3) % NZ, c)
    to_next, to_prev = {"section": (sec + 1) % n_sec}, {"section": (sec + n_sec - 1) % n_sec}

    def zorder(k):
        m = z // 2
        near = m * (3 - z) + (1 - m) * z
        low = 1 - k // 2
        o = low * (k * (1 - near) + (1 - k) * near) + (1 - low) * k
        return m * (3 - o) + (1 - m) * o

    def weight_copies():
        gu, dn = [], []
        for zz in range(NZ):
            for r in range(2):
                cc = c if r == 0 else 1 - c
                for i, (src, dst) in enumerate(((gate_hbm, wg), (up_hbm, wu))):
                    gu.append(pltpu.make_async_copy(src.at[:, zz, cc], dst.at[zz, r], w_sem.at[i, zz, r]))
                for xx in range(NX):
                    col = pl.multiple_of(((xx * NZ + zz) * 2 + cc) * BLK, BLK)
                    dn.append(
                        pltpu.make_async_copy(
                            down_hbm.at[:, pl.ds(col, BLK)],
                            dw.at[zz, r, :, pl.ds(xx * BLK, BLK)],
                            d_sem.at[zz, r, xx],
                        )
                    )
        return gu, dn

    gu_copies, dn_copies = weight_copies()

    bar = pltpu.get_barrier_semaphore()

    def greet(d):
        pl.semaphore_signal(bar, inc=1, device_id=d, device_id_type=MESH)

    for d in (to_sib, to_xp, to_xm):
        greet(d)
    peers = 3
    for cond, d in ((z > 0, to_zm), (z < NZ - 1, to_zp), (sec > 0, to_prev), (sec < n_sec - 1, to_next)):
        pl.when(cond)(functools.partial(greet, d))
        peers = peers + cond.astype(jnp.int32)
    for cp in gu_copies + dn_copies:
        cp.start()
    for t in range(STEPS):
        block = x_ref[:, t, :].astype(F32).T.astype(BF16)
        for h in range(STREAMS):
            xg[h, z, 0, x, pl.ds(t * STOK, STOK)] = block[h * STOK : (h + 1) * STOK]
    for ref in (gate, up, sg):
        ref[...] = jnp.zeros_like(ref)
    pl.semaphore_wait(bar, peers)

    def remote(src, dst, ss, rs, d):
        return pltpu.make_async_remote_copy(
            src_ref=src, dst_ref=dst, send_sem=ss, recv_sem=rs, device_id=d, device_id_type=MESH
        )

    class Gather:
        lags = (0, 2, 4, 5)

        def __init__(self, n, buf, compute, finish):
            self.n, self.buf, self.compute, self.finish = n, buf, compute, finish

        def whole(self, kind, g, xx, d):
            h, zz = g // NZ, zorder(g % NZ)
            ref = self.buf.at[h, zz, 0, xx]
            return remote(ref, ref, ag_ss.at[self.n, kind, g], ag_rm.at[self.n, h * NZ + zz, xx], d)

        def half(self, kind, g, xx, i, d):
            h, zz = g // NZ, zorder(g % NZ)
            ref = self.buf.at[h, zz, 0, xx, pl.ds(i * HALF, HALF)]
            return remote(ref, ref, ag_ss.at[self.n, kind, g], ag_rh.at[self.n, h * NZ + zz, i], d)

        def sib(self, kind, g, xx):
            h, zz = g // NZ, zorder(g % NZ)
            return remote(
                self.buf.at[h, zz, 0, xx], self.buf.at[h, zz, 1, xx],
                ag_ss.at[self.n, kind, g], ag_rs.at[self.n, h * NZ + zz, xx], to_sib,
            )

        def stages(self):
            return self.stage0, self.stage1, self.stage2, self.stage3

        def ups(self, g):
            zz = zorder(g % NZ)
            up_on, down_on = (zz <= z) & (z < NZ - 1), (zz >= z) & (z > 0)
            return (up_on, self.whole(0, g, x, to_zp)), (down_on, self.whole(1, g, x, to_zm))

        def stage0(self, g):
            pl.when(g % NZ > 0)(lambda: self.whole(0, g, x, to_zp).wait_recv())
            self.whole(2, g, x, to_xp).start()
            self.whole(3, g, x, to_xm).start()
            for on, copy in self.ups(g):
                pl.when(on)(copy.start)
            self.sib(4, g, x).start()

        def stage1(self, g):
            self.whole(2, g, xm, to_xp).wait_recv()
            self.half(5, g, xm, 0, to_xp).start()
            self.whole(3, g, xp, to_xm).wait_recv()
            self.half(7, g, xp, 1, to_xm).start()
            self.sib(6, g, xm).start()
            self.sib(8, g, xp).start()

        def stage2(self, g):
            self.half(5, g, xo, 0, to_xp).wait_recv()
            self.half(7, g, xo, 1, to_xm).wait_recv()
            self.sib(9, g, xo).start()

        def stage3(self, g):
            for xx in range(NX):
                self.sib(9, g, xx).wait_recv()
            self.compute(g // NZ, zorder(g % NZ), g)

        def drain(self):
            @pl.loop(0, G)
            def _(g):
                for on, copy in self.ups(g):
                    pl.when(on)(copy.wait_send)
                self.whole(2, g, x, to_xp).wait_send()
                self.whole(3, g, x, to_xm).wait_send()
                self.half(5, g, xm, 0, to_xp).wait_send()
                self.half(7, g, xp, 1, to_xm).wait_send()
                for kind, xx in ((4, x), (6, xm), (8, xp), (9, xo)):
                    self.sib(kind, g, xx).wait_send()

    def gathered(buf, zz, r):
        return jnp.concatenate([buf[zz, r, xx] for xx in range(NX)], axis=1)

    def cols(xx):
        return pl.ds(pl.multiple_of(xx * BLK, BLK), BLK)

    class Scatter:
        lags = (0, 1, 3, 5, 6)

        def __init__(self, n, product, finish):
            self.n, self.product, self.finish = n, product, finish

        def sib(self, g):
            return remote(
                sib_send.at[g], sib_recv.at[self.n, g], rs_ss.at[self.n, 0, g], rs_sib.at[self.n, g], to_sib
            )

        def opp(self, g, i):
            return remote(
                opp_send.at[self.n, g, i], opp_recv.at[self.n, g, i],
                rs_ss.at[self.n, 1 + i, g], rs_opp.at[self.n, g, i], to_xp if i == 0 else to_xm,
            )

        def rl(self, g, i):
            return remote(
                rl_send.at[self.n, g, i], rl_recv.at[self.n, g, i],
                rs_ss.at[self.n, 3 + i, g], rs_rl.at[self.n, g, i], to_xp if i == 0 else to_xm,
            )

        def zcopy(self, g, i):
            slot = (g // NZ) * NZ + zorder(NZ - 1 - g % NZ)
            return remote(
                z_send.at[self.n, g], z_recv.at[self.n, slot, i],
                rs_ss.at[self.n, 5, g], rs_z.at[self.n, slot, i], to_zp if i == 0 else to_zm,
            )

        def stage0(self, g):
            h, zz = g // NZ, zorder(NZ - 1 - g % NZ)
            sib_send[g] = self.product(h, zz, 1).astype(BF16)
            self.sib(g).start()
            acc[g] = self.product(h, zz, 0)

        def stage1(self, g):
            self.sib(g).wait_recv()
            for i in range(2):
                rows = pl.ds(i * HALF, HALF)
                opp_send[self.n, g, i] = (
                    acc[g, rows, cols(xo)] + sib_recv[self.n, g, rows, cols(xo)].astype(F32)
                ).astype(BF16)
                self.opp(g, i).start()

        def stage2(self, g):
            for i in range(2):
                xx = xp if i == 0 else xm
                with_opp, alone = pl.ds(i * HALF, HALF), pl.ds((1 - i) * HALF, HALF)
                rl_send[self.n, g, i, alone] = (
                    acc[g, alone, cols(xx)] + sib_recv[self.n, g, alone, cols(xx)].astype(F32)
                ).astype(BF16)
                part = acc[g, with_opp, cols(xx)] + sib_recv[self.n, g, with_opp, cols(xx)].astype(F32)
                self.opp(g, i).wait_recv()
                rl_send[self.n, g, i, with_opp] = (part + opp_recv[self.n, g, i].astype(F32)).astype(BF16)
                self.rl(g, i).start()

        def stages(self):
            return self.stage0, self.stage1, self.stage2, self.stage3, self.stage4

        def send_on(self, g):
            zz = zorder(NZ - 1 - g % NZ)
            z_send[self.n, g] = tz[g].astype(BF16)
            pl.when(zz > z)(lambda: self.zcopy(g, 0).start())
            pl.when(zz < z)(lambda: self.zcopy(g, 1).start())

        def first_in_line(self, zz):
            return ((zz > z) & (z == 0)) | ((zz < z) & (z == NZ - 1))

        def stage3(self, g):
            zz = zorder(NZ - 1 - g % NZ)
            part = acc[g, :, cols(x)] + sib_recv[self.n, g, :, cols(x)].astype(F32)
            self.rl(g, 0).wait_recv()
            self.rl(g, 1).wait_recv()
            tz[g] = part + (rl_recv[self.n, g, 0].astype(F32) + rl_recv[self.n, g, 1].astype(F32))
            pl.when(self.first_in_line(zz))(lambda: self.send_on(g))

        def stage4(self, g):
            zz = zorder(NZ - 1 - g % NZ)

            def add(i):
                self.zcopy(g, i).wait_recv()
                tz[g] += z_recv[self.n, (g // NZ) * NZ + zz, i].astype(F32)

            pl.when((zz >= z) & (z > 0))(lambda: add(0))
            pl.when((zz <= z) & (z < NZ - 1))(lambda: add(1))
            pl.when((zz > z) & (z > 0) | (zz < z) & (z < NZ - 1))(lambda: self.send_on(g))

        def drain(self):
            @pl.loop(0, G)
            def _(g):
                zz = zorder(NZ - 1 - g % NZ)
                for i in range(2):
                    self.opp(g, i).wait_send()
                    self.rl(g, i).wait_send()
                pl.when(zz > z)(lambda: self.zcopy(g, 0).wait_send())
                pl.when(zz < z)(lambda: self.zcopy(g, 1).wait_send())

    def stage(phase, d, g):
        phase.stages()[d](g)
        if d + 1 == len(phase.lags):
            pl.when(g % NZ == NZ - 1)(lambda: phase.finish(g // NZ))

    def run(cur, prev):
        gap = 0 if prev is None else max(0, prev.lags[-1] - NZ - 1)

        @pl.loop(0, G + gap)
        def _(i):
            if prev is not None:
                for d in reversed(range(1, len(prev.lags))):
                    pl.when(i < prev.lags[d])(lambda d=d: stage(prev, d, i - prev.lags[d] + G))
            for d, lag in enumerate(cur.lags):
                pl.when(i >= lag + gap)(lambda d=d, lag=lag: stage(cur, d, i - lag - gap))

    def finish_last(prev):
        @pl.loop(0, prev.lags[-1])
        def _(i):
            for d in reversed(range(1, len(prev.lags))):
                pl.when(i < prev.lags[d])(lambda d=d: stage(prev, d, i - prev.lags[d] + G))

    def wait_all(copies):
        for cp in copies:
            cp.wait()

    def gate_up(h, zz, g):
        pl.when(g == 0)(lambda: wait_all(gu_copies))
        lhs = jnp.concatenate([gathered(xg.at[h], zz, r) for r in range(2)], axis=1)
        gate[h] += jnp.dot(lhs, wg[zz].reshape(2 * HID, HID), preferred_element_type=F32)
        up[h] += jnp.dot(lhs, wu[zz].reshape(2 * HID, HID), preferred_element_type=F32)

    WIDE = 256

    def tiles(body):
        @pl.loop(0, HID // WIDE)
        def _(i):
            cols = pl.ds(pl.multiple_of(i * WIDE, WIDE), WIDE)
            body([pl.ds(t * STOK, STOK) for t in range(STEPS)], cols)

    def hidden_forward(h):
        def body(rows, cols):
            th = UNIT * hth_ref[:, cols].astype(F32)
            iw = 1.0 / (UNIT * hwd_ref[:, cols].astype(F32))
            p = jnp.zeros((STOK, WIDE), F32)
            s = jnp.zeros((STOK, WIDE), F32)
            for t in range(STEPS):
                g = gate[h, rows[t], cols]
                p = DECAY * (p - th * s) + g * sigmoid(g) * up[h, rows[t], cols]
                s = sigmoid((p - th) * iw)
                spk[h, rows[t], cols] = s
                hs[h, rows[t], cols] = s.astype(BF16)

        tiles(body)

    def projected(h, zz, r):
        return jnp.dot(hs[h], dw[zz, r], preferred_element_type=F32)

    def emit(h):
        return remote(em_send.at[h], em_recv.at[h], sec_s.at[0, h], sec_r.at[0, h], to_next)

    def back(h):
        return remote(ig_send.at[h], ig_recv.at[h], sec_s.at[1, h], sec_r.at[1, h], to_prev)

    def out_stage(h):
        th = UNIT * oth_ref[...].astype(F32)
        iw = 1.0 / (UNIT * owd_ref[...].astype(F32))
        p = jnp.zeros((STOK, BLK), F32)
        s = jnp.zeros((STOK, BLK), F32)
        spikes = []
        for t in range(STEPS):
            rows = pl.ds(t * STOK, STOK)
            p = DECAY * (p - th * s) + (tz[h * NZ + NZ - 1, rows] + xg[h, z, 0, x, rows].astype(F32))
            s = sigmoid((p - th) * iw)
            spikes.append(s)
            em_send[h, rows] = s.astype(BF16)
        dp = jnp.zeros((STOK, BLK), F32)
        for t in reversed(range(STEPS)):
            rows = pl.ds(t * STOK, STOK)
            s = spikes[t]
            ds = cot[h, rows] - (DECAY * th) * dp
            dp = DECAY * dp + ds * (s * (1.0 - s) * iw)
            cgf[h, rows] = dp
            cg[h, z, 0, x, rows] = dp.astype(BF16)
        pl.when(sec < n_sec - 1)(lambda: emit(h).start())

    NT = (((1,), (1,)), ((), ()))

    def spike_grad(h, zz, g):
        for r in range(2):
            sg[h] += lax.dot_general(gathered(cg.at[h], zz, r), dw[zz, r], NT, preferred_element_type=F32)

    def hidden_backward(h):
        def body(rows, cols):
            th = UNIT * hth_ref[:, cols].astype(F32)
            iw = 1.0 / (UNIT * hwd_ref[:, cols].astype(F32))
            dp = jnp.zeros((STOK, WIDE), F32)
            for t in reversed(range(STEPS)):
                s = spk[h, rows[t], cols]
                ds = sg[h, rows[t], cols] - (DECAY * th) * dp
                dp = DECAY * dp + ds * (s * (1.0 - s) * iw)
                g = gate[h, rows[t], cols]
                q = sigmoid(g)
                ug[h, rows[t], cols] = (dp * (g * q)).astype(BF16)
                gg[h, rows[t], cols] = (dp * up[h, rows[t], cols] * (q * (1.0 + g * (1.0 - q)))).astype(BF16)

        tiles(body)

    def input_grad(h, zz, r):
        return lax.dot_general(
            gg[h], wg[zz, r].reshape(HID, HID), NT, preferred_element_type=F32
        ) + lax.dot_general(ug[h], wu[zz, r].reshape(HID, HID), NT, preferred_element_type=F32)

    def last_stage(h):
        ig_send[h] = (tz[h * NZ + NZ - 1] + cgf[h]).astype(BF16)
        pl.when(sec > 0)(lambda: back(h).start())

    def before_down(h):
        hidden_forward(h)
        pl.when(h == 0)(lambda: wait_all(dn_copies))

    gather1, gather2 = Gather(0, xg, gate_up, before_down), Gather(1, cg, spike_grad, hidden_backward)
    scatter1, scatter2 = Scatter(0, projected, out_stage), Scatter(1, input_grad, last_stage)

    def sib_sent(phase):
        @pl.loop(0, G)
        def _(g):
            phase.sib(g).wait_send()

    run(gather1, None)
    for t in range(STEPS):
        block = cot_ref[:, t, :].astype(F32).T
        for h in range(STREAMS):
            cot[h, pl.ds(t * STOK, STOK)] = block[h * STOK : (h + 1) * STOK]
    run(scatter1, gather1)
    run(gather2, scatter1)
    sib_sent(scatter1)
    run(scatter2, gather2)
    finish_last(scatter2)
    sib_sent(scatter2)

    def restore(ref, recv):
        for t in range(STEPS):
            rows = jnp.concatenate([recv[h, pl.ds(t * STOK, STOK)] for h in range(STREAMS)], axis=0)
            ref[:, t, :] = rows.astype(F32).T.astype(BF16)

    def clear(ref):
        ref[...] = jnp.zeros_like(ref)

    @pl.when(sec > 0)
    def _():
        for h in range(STREAMS):
            emit(h).wait_recv()
        restore(inc_ref, em_recv)

    pl.when(sec == 0)(lambda: clear(inc_ref))
    for phase in (gather1, scatter1, gather2, scatter2):
        phase.drain()
    for h in range(STREAMS):
        pl.when(sec < n_sec - 1)(emit(h).wait_send)
        pl.when(sec > 0)(back(h).wait_send)

    @pl.when(sec < n_sec - 1)
    def _():
        for h in range(STREAMS):
            back(h).wait_recv()
        restore(ret_ref, ig_recv)

    pl.when(sec == n_sec - 1)(lambda: clear(ret_ref))


def per_device(layer_input, gate_w, up_w, down_w, hth, hwd, oth, owd, cotangent):
    vmem, hbm, dma = pltpu.VMEM, pl.BlockSpec(memory_space=pl.ANY), pltpu.SemaphoreType.DMA
    local = pl.BlockSpec(memory_space=pltpu.VMEM)
    blocked = (NX, NZ, 2, BLK, HID)
    incoming, returned = pl.pallas_call(
        kernel,
        out_shape=(jax.ShapeDtypeStruct((BLK, STEPS, TOK), BF16),) * 2,
        in_specs=[local] * 6 + [hbm] * 3,
        out_specs=(local, local),
        scratch_shapes=[
            vmem((NZ, 2, NX, BLK, HID), BF16),
            vmem((NZ, 2, NX, BLK, HID), BF16),
            vmem((NZ, 2, HID, NX * BLK), BF16),
            vmem((STREAMS, NZ, 2, NX, SROWS, BLK), BF16),
            vmem((STREAMS, NZ, 2, NX, SROWS, BLK), BF16),
            vmem((STREAMS, SROWS, HID), F32),
            vmem((STREAMS, SROWS, HID), F32),
            vmem((STREAMS, SROWS, HID), F32),
            vmem((STREAMS, SROWS, HID), BF16),
            vmem((STREAMS, SROWS, HID), F32),
            vmem((STREAMS, SROWS, HID), BF16),
            vmem((STREAMS, SROWS, HID), BF16),
            vmem((G, SROWS, BLK), F32),
            vmem((STREAMS, SROWS, BLK), F32),
            vmem((STREAMS, SROWS, BLK), F32),
            vmem((G, SROWS, NX * BLK), F32),
            vmem((G, SROWS, NX * BLK), BF16),
            vmem((2, G, 2, HALF, BLK), BF16),
            vmem((2, G, 2, SROWS, BLK), BF16),
            vmem((2, G, SROWS, BLK), BF16),
            vmem((2, G, SROWS, NX * BLK), BF16),
            vmem((2, G, 2, HALF, BLK), BF16),
            vmem((2, G, 2, SROWS, BLK), BF16),
            vmem((2, G, 2, SROWS, BLK), BF16),
            vmem((STREAMS, SROWS, BLK), BF16),
            vmem((STREAMS, SROWS, BLK), BF16),
            vmem((STREAMS, SROWS, BLK), BF16),
            vmem((STREAMS, SROWS, BLK), BF16),
            dma((2, NZ, 2)),
            dma((NZ, 2, NX)),
            dma((2, 10, G)),
            dma((2, G, NX)),
            dma((2, G, 2)),
            dma((2, G, NX)),
            dma((2, 6, G)),
            dma((2, G)),
            dma((2, G, 2)),
            dma((2, G, 2)),
            dma((2, G, 2)),
            dma((2, STREAMS)),
            dma((2, STREAMS)),
        ],
        compiler_params=pltpu.CompilerParams(
            collective_id=0, has_side_effects=True, vmem_limit_bytes=60 * 2**20
        ),
        cost_estimate=pl.CostEstimate(
            flops=12 * ROWS * HID * 4096, bytes_accessed=12 * 2**20, transcendentals=2**20
        ),
        name="layer",
    )(
        layer_input[0], cotangent[0], hth, hwd, oth, owd,
        gate_w.reshape(blocked), up_w.reshape(blocked), down_w.reshape(HID, -1),
    )
    return incoming[None], returned[None]


def solution(mesh):
    placed = (
        P("section", "dp", None, None),
        P("section", None, "dp"),
        P("section", None, "dp"),
        P("section", "dp", None),
        P("section", "dp"),
        P("section", "dp"),
        P("section", "dp"),
        P("section", "dp"),
        P("section", "dp", None, None),
    )
    return jax.shard_map(
        per_device,
        mesh=mesh,
        in_specs=placed,
        out_specs=(P("section", "dp", None, None), P("section", "dp", None, None)),
        check_vma=False,
    )
```

time: 517 us -> 126 us (0.24)
  waiting for transfers between devices: 448 us -> 0 us
  Pallas kernels: 0 us -> 122 us
  matrix products: 27.9 us -> 0 us
  between operations: 14 us -> 0.64 us
  starting transfers between devices: 9.46 us -> 0 us
  local copies, waits for them, and re-layouts: 10.9 us -> 3.21 us
  other arithmetic: 6.69 us -> 0 us
    reduce_scatter x1 -> x0, waiting for transfers between devices: 159 us -> none  [per_device(): lax.psum_scatter(contract(part, spikes, 0, 1), 'dp', scatter_dimension=0,...]
    unnamed x5 -> x0, waiting for transfers between devices: 146 us -> none
    all_gather x2 -> x0, waiting for transfers between devices: 133 us -> none  [the longest x1 66.9 us: per_device(): piece = lax.all_gather(grad_block, 'dp', axis=1, tiled=True)]
    pallas_call x0 -> x1, Pallas kernels: none -> 122 us  [per_device(): pl.pallas_call(kernel, out_shape=(jax.ShapeDtypeStruct((BLK, STEPS, TOK),...]
    dot_general x6 -> x0, matrix products: 27.9 us -> none  [contract(): lax.dot_general(left, right, (((left_dim,), (right_dim,)), ((), ())), pre...]
    ppermute x2 -> x0, waiting for transfers between devices: 10.2 us -> none  [the longest x1 10.2 us: with_halo(): lax.ppermute(lax.slice_in_dim(block, 0, width, axis=dim), axis, backward)]
    ppermute x2 -> x0, starting transfers between devices: 9.12 us -> none  [the longest x1 6.45 us: with_halo(): lax.ppermute(lax.slice_in_dim(block, block.shape[dim] - width, None, axis...]
    unnamed x24 -> x2, local copies, waits for them, and re-layouts: 10.3 us -> 3.21 us
  transfers between devices with their start and end apart: 6 -> 0, of which waited for: 5 -> 0; matrix products, arithmetic and copies ran while one was open for 1% -> 0% of each run, Pallas kernels for 0% -> 0%
where the time goes in v2:
time: 126 us
  Pallas kernels  122 us (97%)
  local copies, waits for them, and re-layouts  3.21 us (3%)
    pallas_call x1, Pallas kernels, per_device(): pl.pallas_call(kernel, out_shape=(jax.ShapeDtypeStruct((BLK, STEPS, TOK),...  122 us
    unnamed x2, local copies, waits for them, and re-layouts  3.21 us

profile of v2, /device:TPU:24, one launch (start us, length us, event | category | flops | bytes accessed | tf_op | source)
XLA Modules:
  0.0 126.1 jit_solution(16436928847073020834)
XLA Ops:
  0.6 122.2 %layer.1 = (bf16[128,4,128]{2,1,0:T(4,128)(2,1)}, bf16[128,4,128]{2,1,0:T(4,128)(2,1)}) custom-call(bf16[128,4,128]{2,1,0:T(4,128)(2,1)} %bitcast.12, bf16[128,4,128]{2,1,0:T(4,128)(2,1)} %bitcast.13, s32[1,512]{1,0:T(1,128)} %hth_ref.1, s32[1,512]{1,0:T(1,128)} %hwd_ref.1, s32[1,128]{1,0:T(1,128)} %oth_ref.1, s32[1,128]{1,0:T(1,128)} %owd_ref.1, ...), custom_call_target="tpu_custom_call" | custom-call | flops 12884901888 | bytes 12582912 | tf_op jit(solution)/shard_map/layer/pallas_call | solution.py:454
  122.9 1.6 %copy.13 = bf16[1,128,4,128]{3,2,1,0:T(4,128)(2,1)} copy(bf16[1,128,4,128]{3,2,1,0:T(4,128)(2,1)} %bitcast.8) | data formatting | bytes 262144
  124.5 1.6 %copy.14 = bf16[1,128,4,128]{3,2,1,0:T(4,128)(2,1)} copy(bf16[1,128,4,128]{3,2,1,0:T(4,128)(2,1)} %bitcast.7) | data formatting | bytes 262144

commit v3 on v2

--- a/solution.py
+++ b/solution.py
@@ -32,8 +32,8 @@
     inc_ref, ret_ref,
     wg, wu, dw, xg, cg, gate, up, spk, hs, sg, gg, ug, tz, cgf,
     cot, acc, sib_send, opp_send, rl_send, z_send,
-    sib_recv, opp_recv, rl_recv, z_recv, em_send, ig_send, em_recv, ig_recv,
-    w_sem, d_sem, ag_ss, ag_rm, ag_rh, ag_rs, rs_ss, rs_sib, rs_opp, rs_rl, rs_z, sec_s, sec_r,
+    sib_recv, opp_recv, rl_recv, z_recv, em_send, ig_send,
+    w_sem, d_sem, ag_ss, ag_rz, ag_rx, ag_rh, ag_rs, rs_ss, rs_sib, rs_opp, rs_rl, rs_z, sec_s, sec_r,
 ):
     me = lax.axis_index("dp")
     sec = lax.axis_index("section")
@@ -47,7 +47,10 @@
 
     xp, xm, xo = (x + 1) % NX, (x + 3) % NX, (x + 2) % NX
     to_sib, to_xp, to_xm = dev(x, z, 1 - c), dev(xp, z, c), dev(xm, z, c)
-    to_zp, to_zm = dev(x, (z + 1) % NZ, c), dev(x, (z + 3) % NZ, c)
+
+    def to_z(j):
+        return dev(x, (z + j) % NZ, c)
+
     to_next, to_prev = {"section": (sec + 1) % n_sec}, {"section": (sec + n_sec - 1) % n_sec}
 
     def zorder(k):
@@ -82,10 +85,10 @@
     def greet(d):
         pl.semaphore_signal(bar, inc=1, device_id=d, device_id_type=MESH)
 
-    for d in (to_sib, to_xp, to_xm):
+    for d in (to_sib, to_xp, to_xm) + tuple(to_z(j) for j in range(1, NZ)):
         greet(d)
-    peers = 3
-    for cond, d in ((z > 0, to_zm), (z < NZ - 1, to_zp), (sec > 0, to_prev), (sec < n_sec - 1, to_next)):
+    peers = 3 + NZ - 1
+    for cond, d in ((sec > 0, to_prev), (sec < n_sec - 1, to_next)):
         pl.when(cond)(functools.partial(greet, d))
         peers = peers + cond.astype(jnp.int32)
     for cp in gu_copies + dn_copies:
@@ -109,68 +112,65 @@
         def __init__(self, n, buf, compute, finish):
             self.n, self.buf, self.compute, self.finish = n, buf, compute, finish
 
-        def whole(self, kind, g, xx, d):
+        def at(self, g):
             h, zz = g // NZ, zorder(g % NZ)
-            ref = self.buf.at[h, zz, 0, xx]
-            return remote(ref, ref, ag_ss.at[self.n, kind, g], ag_rm.at[self.n, h * NZ + zz, xx], d)
-
-        def half(self, kind, g, xx, i, d):
-            h, zz = g // NZ, zorder(g % NZ)
-            ref = self.buf.at[h, zz, 0, xx, pl.ds(i * HALF, HALF)]
-            return remote(ref, ref, ag_ss.at[self.n, kind, g], ag_rh.at[self.n, h * NZ + zz, i], d)
-
-        def sib(self, kind, g, xx):
-            h, zz = g // NZ, zorder(g % NZ)
-            return remote(
-                self.buf.at[h, zz, 0, xx], self.buf.at[h, zz, 1, xx],
-                ag_ss.at[self.n, kind, g], ag_rs.at[self.n, h * NZ + zz, xx], to_sib,
-            )
+            return self.buf.at[h, zz], h * NZ + zz
+
+        def along_z(self, h, j):
+            ref = self.buf.at[h, z, 0, x]
+            return remote(ref, ref, ag_ss.at[self.n, 0], ag_rz.at[self.n, h * NZ + z], to_z(j))
+
+        def whole(self, g, d):
+            ref, slot = self.at(g)
+            return remote(ref.at[0, x], ref.at[0, x], ag_ss.at[self.n, 1], ag_rx.at[self.n, slot], d)
+
+        def half(self, g, xx, i, d):
+            ref, slot = self.at(g)
+            ref = ref.at[0, xx, pl.ds(i * HALF, HALF)]
+            return remote(ref, ref, ag_ss.at[self.n, 2], ag_rh.at[self.n, slot], d)
+
+        def sib(self, g):
+            ref, slot = self.at(g)
+            return remote(ref.at[0], ref.at[1], ag_ss.at[self.n, 3], ag_rs.at[self.n, slot], to_sib)
+
+        def arrived(self, blocks, sem):
+            ref = self.buf.at[0, 0, 0, pl.ds(0, blocks)]
+            remote(ref, ref, ag_ss.at[self.n, 0], sem, to_sib).wait_recv()
+
+        def spread(self, h):
+            for j in (2, 1, 3):
+                self.along_z(h, j).start()
+
+        def stage0(self, g):
+            pl.when(g % NZ > 0)(lambda: self.arrived(1, ag_rz.at[self.n, self.at(g)[1]]))
+            self.whole(g, to_xp).start()
+            self.whole(g, to_xm).start()
+
+        def stage1(self, g):
+            self.arrived(2, ag_rx.at[self.n, self.at(g)[1]])
+            self.half(g, xm, 0, to_xp).start()
+            self.half(g, xp, 1, to_xm).start()
+
+        def stage2(self, g):
+            self.arrived(1, ag_rh.at[self.n, self.at(g)[1]])
+            self.sib(g).start()
+
+        def stage3(self, g):
+            self.sib(g).wait_recv()
+            self.compute(g // NZ, zorder(g % NZ), g)
 
         def stages(self):
             return self.stage0, self.stage1, self.stage2, self.stage3
 
-        def ups(self, g):
-            zz = zorder(g % NZ)
-            up_on, down_on = (zz <= z) & (z < NZ - 1), (zz >= z) & (z > 0)
-            return (up_on, self.whole(0, g, x, to_zp)), (down_on, self.whole(1, g, x, to_zm))
-
-        def stage0(self, g):
-            pl.when(g % NZ > 0)(lambda: self.whole(0, g, x, to_zp).wait_recv())
-            self.whole(2, g, x, to_xp).start()
-            self.whole(3, g, x, to_xm).start()
-            for on, copy in self.ups(g):
-                pl.when(on)(copy.start)
-            self.sib(4, g, x).start()
-
-        def stage1(self, g):
-            self.whole(2, g, xm, to_xp).wait_recv()
-            self.half(5, g, xm, 0, to_xp).start()
-            self.whole(3, g, xp, to_xm).wait_recv()
-            self.half(7, g, xp, 1, to_xm).start()
-            self.sib(6, g, xm).start()
-            self.sib(8, g, xp).start()
-
-        def stage2(self, g):
-            self.half(5, g, xo, 0, to_xp).wait_recv()
-            self.half(7, g, xo, 1, to_xm).wait_recv()
-            self.sib(9, g, xo).start()
-
-        def stage3(self, g):
-            for xx in range(NX):
-                self.sib(9, g, xx).wait_recv()
-            self.compute(g // NZ, zorder(g % NZ), g)
-
         def drain(self):
-            @pl.loop(0, G)
-            def _(g):
-                for on, copy in self.ups(g):
-                    pl.when(on)(copy.wait_send)
-                self.whole(2, g, x, to_xp).wait_send()
-                self.whole(3, g, x, to_xm).wait_send()
-                self.half(5, g, xm, 0, to_xp).wait_send()
-                self.half(7, g, xp, 1, to_xm).wait_send()
-                for kind, xx in ((4, x), (6, xm), (8, xp), (9, xo)):
-                    self.sib(kind, g, xx).wait_send()
+            def sent(ref, kind):
+                remote(ref, ref, ag_ss.at[self.n, kind], ag_rz.at[self.n, 0], to_sib).wait_send()
+
+            for _ in range(STREAMS):
+                sent(self.buf.at[0, 0, 0, pl.ds(0, NZ - 1)], 0)
+            sent(self.buf.at[pl.ds(0, STREAMS // 2), :, 0], 1)
+            sent(self.buf.at[:, 0, 0], 2)
+            sent(self.buf.at[:, :, 0], 3)
 
     def gathered(buf, zz, r):
         return jnp.concatenate([buf[zz, r, xx] for xx in range(NX)], axis=1)
@@ -186,26 +186,29 @@
 
         def sib(self, g):
             return remote(
-                sib_send.at[g], sib_recv.at[self.n, g], rs_ss.at[self.n, 0, g], rs_sib.at[self.n, g], to_sib
+                sib_send.at[g], sib_recv.at[self.n, g], rs_ss.at[self.n, 0], rs_sib.at[self.n, g], to_sib
             )
 
         def opp(self, g, i):
             return remote(
                 opp_send.at[self.n, g, i], opp_recv.at[self.n, g, i],
-                rs_ss.at[self.n, 1 + i, g], rs_opp.at[self.n, g, i], to_xp if i == 0 else to_xm,
+                rs_ss.at[self.n, 1], rs_opp.at[self.n, g], to_xp if i == 0 else to_xm,
             )
 
         def rl(self, g, i):
             return remote(
                 rl_send.at[self.n, g, i], rl_recv.at[self.n, g, i],
-                rs_ss.at[self.n, 3 + i, g], rs_rl.at[self.n, g, i], to_xp if i == 0 else to_xm,
+                rs_ss.at[self.n, 2], rs_rl.at[self.n, g], to_xp if i == 0 else to_xm,
             )
 
-        def zcopy(self, g, i):
-            slot = (g // NZ) * NZ + zorder(NZ - 1 - g % NZ)
+        def both(self, recv, sem):
+            remote(recv, recv, rs_ss.at[self.n, 0], sem, to_sib).wait_recv()
+
+        def zcopy(self, g, source, target):
+            h = g // NZ
             return remote(
-                z_send.at[self.n, g], z_recv.at[self.n, slot, i],
-                rs_ss.at[self.n, 5, g], rs_z.at[self.n, slot, i], to_zp if i == 0 else to_zm,
+                z_send.at[self.n, g], z_recv.at[self.n, h * NZ + source],
+                rs_ss.at[self.n, 3], rs_z.at[self.n, h], dev(x, target, c),
             )
 
         def stage0(self, g):
@@ -224,6 +227,7 @@
                 self.opp(g, i).start()
 
         def stage2(self, g):
+            self.both(opp_recv.at[self.n, g], rs_opp.at[self.n, g])
             for i in range(2):
                 xx = xp if i == 0 else xm
                 with_opp, alone = pl.ds(i * HALF, HALF), pl.ds((1 - i) * HALF, HALF)
@@ -231,50 +235,43 @@
                     acc[g, alone, cols(xx)] + sib_recv[self.n, g, alone, cols(xx)].astype(F32)
                 ).astype(BF16)
                 part = acc[g, with_opp, cols(xx)] + sib_recv[self.n, g, with_opp, cols(xx)].astype(F32)
-                self.opp(g, i).wait_recv()
                 rl_send[self.n, g, i, with_opp] = (part + opp_recv[self.n, g, i].astype(F32)).astype(BF16)
                 self.rl(g, i).start()
 
         def stages(self):
             return self.stage0, self.stage1, self.stage2, self.stage3, self.stage4
 
-        def send_on(self, g):
-            zz = zorder(NZ - 1 - g % NZ)
-            z_send[self.n, g] = tz[g].astype(BF16)
-            pl.when(zz > z)(lambda: self.zcopy(g, 0).start())
-            pl.when(zz < z)(lambda: self.zcopy(g, 1).start())
-
-        def first_in_line(self, zz):
-            return ((zz > z) & (z == 0)) | ((zz < z) & (z == NZ - 1))
-
         def stage3(self, g):
-            zz = zorder(NZ - 1 - g % NZ)
             part = acc[g, :, cols(x)] + sib_recv[self.n, g, :, cols(x)].astype(F32)
-            self.rl(g, 0).wait_recv()
-            self.rl(g, 1).wait_recv()
-            tz[g] = part + (rl_recv[self.n, g, 0].astype(F32) + rl_recv[self.n, g, 1].astype(F32))
-            pl.when(self.first_in_line(zz))(lambda: self.send_on(g))
+            self.both(rl_recv.at[self.n, g], rs_rl.at[self.n, g])
+            part = part + (rl_recv[self.n, g, 0].astype(F32) + rl_recv[self.n, g, 1].astype(F32))
+
+            @pl.when(g % NZ < NZ - 1)
+            def _():
+                z_send[self.n, g] = part.astype(BF16)
+                self.zcopy(g, z, zorder(NZ - 1 - g % NZ)).start()
+
+            @pl.when(g % NZ == NZ - 1)
+            def _():
+                tz[g // NZ] = part
 
         def stage4(self, g):
-            zz = zorder(NZ - 1 - g % NZ)
-
-            def add(i):
-                self.zcopy(g, i).wait_recv()
-                tz[g] += z_recv[self.n, (g // NZ) * NZ + zz, i].astype(F32)
-
-            pl.when((zz >= z) & (z > 0))(lambda: add(0))
-            pl.when((zz <= z) & (z < NZ - 1))(lambda: add(1))
-            pl.when((zz > z) & (z > 0) | (zz < z) & (z < NZ - 1))(lambda: self.send_on(g))
+            @pl.when(g % NZ == NZ - 1)
+            def _():
+                h = g // NZ
+                self.both(z_recv.at[self.n, pl.ds(0, NZ - 1)], rs_z.at[self.n, h])
+                total = tz[h]
+                for j in range(1, NZ):
+                    total += z_recv[self.n, h * NZ + (z + j) % NZ].astype(F32)
+                tz[h] = total
+
+        def sent(self, ref, kind):
+            remote(ref, ref, rs_ss.at[self.n, kind], rs_sib.at[self.n, 0], to_sib).wait_send()
 
         def drain(self):
-            @pl.loop(0, G)
-            def _(g):
-                zz = zorder(NZ - 1 - g % NZ)
-                for i in range(2):
-                    self.opp(g, i).wait_send()
-                    self.rl(g, i).wait_send()
-                pl.when(zz > z)(lambda: self.zcopy(g, 0).wait_send())
-                pl.when(zz < z)(lambda: self.zcopy(g, 1).wait_send())
+            self.sent(opp_send.at[self.n], 1)
+            self.sent(rl_send.at[self.n], 2)
+            self.sent(z_send.at[self.n, pl.ds(0, STREAMS * (NZ - 1))], 3)
 
     def stage(phase, d, g):
         phase.stages()[d](g)
@@ -282,7 +279,7 @@
             pl.when(g % NZ == NZ - 1)(lambda: phase.finish(g // NZ))
 
     def run(cur, prev):
-        gap = 0 if prev is None else max(0, prev.lags[-1] - NZ - 1)
+        gap = 0 if prev is None else max(0, prev.lags[-1] + NZ - 1 - G)
 
         @pl.loop(0, G + gap)
         def _(i):
@@ -335,10 +332,10 @@
         return jnp.dot(hs[h], dw[zz, r], preferred_element_type=F32)
 
     def emit(h):
-        return remote(em_send.at[h], em_recv.at[h], sec_s.at[0, h], sec_r.at[0, h], to_next)
+        return remote(em_send.at[h], inc_ref.at[h], sec_s.at[0, h], sec_r.at[0, h], to_next)
 
     def back(h):
-        return remote(ig_send.at[h], ig_recv.at[h], sec_s.at[1, h], sec_r.at[1, h], to_prev)
+        return remote(ig_send.at[h], ret_ref.at[h], sec_s.at[1, h], sec_r.at[1, h], to_prev)
 
     def out_stage(h):
         th = UNIT * oth_ref[...].astype(F32)
@@ -348,7 +345,7 @@
         spikes = []
         for t in range(STEPS):
             rows = pl.ds(t * STOK, STOK)
-            p = DECAY * (p - th * s) + (tz[h * NZ + NZ - 1, rows] + xg[h, z, 0, x, rows].astype(F32))
+            p = DECAY * (p - th * s) + (tz[h, rows] + xg[h, z, 0, x, rows].astype(F32))
             s = sigmoid((p - th) * iw)
             spikes.append(s)
             em_send[h, rows] = s.astype(BF16)
@@ -360,6 +357,7 @@
             dp = DECAY * dp + ds * (s * (1.0 - s) * iw)
             cgf[h, rows] = dp
             cg[h, z, 0, x, rows] = dp.astype(BF16)
+        gather2.spread(h)
         pl.when(sec < n_sec - 1)(lambda: emit(h).start())
 
     NT = (((1,), (1,)), ((), ()))
@@ -390,7 +388,7 @@
         ) + lax.dot_general(ug[h], wu[zz, r].reshape(HID, HID), NT, preferred_element_type=F32)
 
     def last_stage(h):
-        ig_send[h] = (tz[h * NZ + NZ - 1] + cgf[h]).astype(BF16)
+        ig_send[h] = (tz[h] + cgf[h]).astype(BF16)
         pl.when(sec > 0)(lambda: back(h).start())
 
     def before_down(h):
@@ -400,11 +398,8 @@
     gather1, gather2 = Gather(0, xg, gate_up, before_down), Gather(1, cg, spike_grad, hidden_backward)
     scatter1, scatter2 = Scatter(0, projected, out_stage), Scatter(1, input_grad, last_stage)
 
-    def sib_sent(phase):
-        @pl.loop(0, G)
-        def _(g):
-            phase.sib(g).wait_send()
-
+    for h in range(STREAMS):
+        gather1.spread(h)
     run(gather1, None)
     for t in range(STEPS):
         block = cot_ref[:, t, :].astype(F32).T
@@ -412,15 +407,10 @@
             cot[h, pl.ds(t * STOK, STOK)] = block[h * STOK : (h + 1) * STOK]
     run(scatter1, gather1)
     run(gather2, scatter1)
-    sib_sent(scatter1)
+    scatter1.sent(sib_send, 0)
     run(scatter2, gather2)
     finish_last(scatter2)
-    sib_sent(scatter2)
-
-    def restore(ref, recv):
-        for t in range(STEPS):
-            rows = jnp.concatenate([recv[h, pl.ds(t * STOK, STOK)] for h in range(STREAMS)], axis=0)
-            ref[:, t, :] = rows.astype(F32).T.astype(BF16)
+    scatter2.sent(sib_send, 0)
 
     def clear(ref):
         ref[...] = jnp.zeros_like(ref)
@@ -429,7 +419,6 @@
     def _():
         for h in range(STREAMS):
             emit(h).wait_recv()
-        restore(inc_ref, em_recv)
 
     pl.when(sec == 0)(lambda: clear(inc_ref))
     for phase in (gather1, scatter1, gather2, scatter2):
@@ -442,9 +431,15 @@
     def _():
         for h in range(STREAMS):
             back(h).wait_recv()
-        restore(ret_ref, ig_recv)
 
     pl.when(sec == n_sec - 1)(lambda: clear(ret_ref))
+
+
+def turn(inc_rows, ret_rows, inc_ref, ret_ref):
+    for rows, ref in ((inc_rows, inc_ref), (ret_rows, ret_ref)):
+        for t in range(STEPS):
+            block = jnp.concatenate([rows[h, pl.ds(t * STOK, STOK)] for h in range(STREAMS)], axis=0)
+            ref[:, t, :] = block.astype(F32).T.astype(BF16)
 
 
 def per_device(layer_input, gate_w, up_w, down_w, hth, hwd, oth, owd, cotangent):
@@ -453,7 +448,7 @@
     blocked = (NX, NZ, 2, BLK, HID)
     incoming, returned = pl.pallas_call(
         kernel,
-        out_shape=(jax.ShapeDtypeStruct((BLK, STEPS, TOK), BF16),) * 2,
+        out_shape=(jax.ShapeDtypeStruct((STREAMS, SROWS, BLK), BF16),) * 2,
         in_specs=[local] * 6 + [hbm] * 3,
         out_specs=(local, local),
         scratch_shapes=[
@@ -469,7 +464,7 @@
             vmem((STREAMS, SROWS, HID), F32),
             vmem((STREAMS, SROWS, HID), BF16),
             vmem((STREAMS, SROWS, HID), BF16),
-            vmem((G, SROWS, BLK), F32),
+            vmem((STREAMS, SROWS, BLK), F32),
             vmem((STREAMS, SROWS, BLK), F32),
             vmem((STREAMS, SROWS, BLK), F32),
             vmem((G, SROWS, NX * BLK), F32),
@@ -480,22 +475,21 @@
             vmem((2, G, SROWS, NX * BLK), BF16),
             vmem((2, G, 2, HALF, BLK), BF16),
             vmem((2, G, 2, SROWS, BLK), BF16),
-            vmem((2, G, 2, SROWS, BLK), BF16),
-            vmem((STREAMS, SROWS, BLK), BF16),
-            vmem((STREAMS, SROWS, BLK), BF16),
+            vmem((2, G, SROWS, BLK), BF16),
             vmem((STREAMS, SROWS, BLK), BF16),
             vmem((STREAMS, SROWS, BLK), BF16),
             dma((2, NZ, 2)),
             dma((NZ, 2, NX)),
-            dma((2, 10, G)),
-            dma((2, G, NX)),
-            dma((2, G, 2)),
-            dma((2, G, NX)),
-            dma((2, 6, G)),
-            dma((2, G)),
-            dma((2, G, 2)),
-            dma((2, G, 2)),
-            dma((2, G, 2)),
+            dma((2, 4)),
+            dma((2, G)),
+            dma((2, G)),
+            dma((2, G)),
+            dma((2, G)),
+            dma((2, 4)),
+            dma((2, G)),
+            dma((2, G)),
+            dma((2, G)),
+            dma((2, STREAMS)),
             dma((2, STREAMS)),
             dma((2, STREAMS)),
         ],
@@ -510,6 +504,13 @@
         layer_input[0], cotangent[0], hth, hwd, oth, owd,
         gate_w.reshape(blocked), up_w.reshape(blocked), down_w.reshape(HID, -1),
     )
+    incoming, returned = pl.pallas_call(
+        turn,
+        out_shape=(jax.ShapeDtypeStruct((BLK, STEPS, TOK), BF16),) * 2,
+        in_specs=[local] * 2,
+        out_specs=(local, local),
+        name="turn",
+    )(incoming, returned)
     return incoming[None], returned[None]
 
 

time: 126 us -> 114 us (0.905); the launches traced: 126 us -> 113 us
  Pallas kernels: 122 us -> 112 us
  local copies, waits for them, and re-layouts: 3.21 us -> 0 us
    pallas_call x1 -> x2, Pallas kernels: 122 us -> 112 us  [the longest x1 110 us: per_device(): pl.pallas_call(kernel, out_shape=(jax.ShapeDtypeStruct((STREAMS, SROWS, B...]
    unnamed x2 -> x0, local copies, waits for them, and re-layouts: 3.21 us -> none
where the time goes in v3:
time: 114 us; the launch traced here: 113 us
  Pallas kernels  112 us (98%)
    pallas_call x1, Pallas kernels, per_device(): pl.pallas_call(kernel, out_shape=(jax.ShapeDtypeStruct((STREAMS, SROWS, B...  110 us
    pallas_call x1, Pallas kernels, per_device(): pl.pallas_call(turn, out_shape=(jax.ShapeDtypeStruct((BLK, STEPS, TOK), B...  2.44 us

profile of v3, /device:TPU:24, one launch (start us, length us, event | category | flops | bytes accessed | tf_op | source)
XLA Modules:
  0.0 112.7 jit_solution(13903230225916674693)
XLA Ops:
  0.6 109.6 %layer.1 = (bf16[2,256,128]{2,1,0:T(8,128)(2,1)}, bf16[2,256,128]{2,1,0:T(8,128)(2,1)}) custom-call(bf16[128,4,128]{2,1,0:T(4,128)(2,1)} %bitcast.10, bf16[128,4,128]{2,1,0:T(4,128)(2,1)} %bitcast.11, s32[1,512]{1,0:T(1,128)} %hth_ref.1, s32[1,512]{1,0:T(1,128)} %hwd_ref.1, s32[1,128]{1,0:T(1,128)} %oth_ref.1, s32[1,128]{1,0:T(1,128)} %owd_ref.1, ...), custom_call_target="tpu_custom_call" | custom-call | flops 12884901888 | bytes 12582912 | tf_op jit(solution)/shard_map/layer/pallas_call | solution.py:449
  110.3 2.4 %turn.1 = (bf16[128,4,128]{2,1,0:T(4,128)(2,1)}, bf16[128,4,128]{2,1,0:T(4,128)(2,1)}) custom-call(bf16[2,256,128]{2,1,0:T(8,128)(2,1)} %get-tuple-element.6.inc_rows, bf16[2,256,128]{2,1,0:T(8,128)(2,1)} %get-tuple-element.7.ret_rows), custom_call_target="tpu_custom_call" | custom-call | tf_op jit(solution)/shard_map/turn/pallas_call | solution.py:507

commit v4 on v3

--- a/solution.py
+++ b/solution.py
@@ -108,6 +108,8 @@
 
     class Gather:
         lags = (0, 2, 4, 5)
+        order = (1, 2, 0, 3)
+        late_order = (1, 2, 3)
 
         def __init__(self, n, buf, compute, finish):
             self.n, self.buf, self.compute, self.finish = n, buf, compute, finish
@@ -179,7 +181,9 @@
         return pl.ds(pl.multiple_of(xx * BLK, BLK), BLK)
 
     class Scatter:
-        lags = (0, 1, 3, 5, 6)
+        lags = (0, 1, 3, 4)
+        order = (2, 1, 0, 3)
+        late_order = (2, 1, 3)
 
         def __init__(self, n, product, finish):
             self.n, self.product, self.finish = n, product, finish
@@ -239,7 +243,7 @@
                 self.rl(g, i).start()
 
         def stages(self):
-            return self.stage0, self.stage1, self.stage2, self.stage3, self.stage4
+            return self.stage0, self.stage1, self.stage2, self.stage3
 
         def stage3(self, g):
             part = acc[g, :, cols(x)] + sib_recv[self.n, g, :, cols(x)].astype(F32)
@@ -253,14 +257,9 @@
 
             @pl.when(g % NZ == NZ - 1)
             def _():
-                tz[g // NZ] = part
-
-        def stage4(self, g):
-            @pl.when(g % NZ == NZ - 1)
-            def _():
                 h = g // NZ
                 self.both(z_recv.at[self.n, pl.ds(0, NZ - 1)], rs_z.at[self.n, h])
-                total = tz[h]
+                total = part
                 for j in range(1, NZ):
                     total += z_recv[self.n, h * NZ + (z + j) % NZ].astype(F32)
                 tz[h] = total
@@ -284,15 +283,16 @@
         @pl.loop(0, G + gap)
         def _(i):
             if prev is not None:
-                for d in reversed(range(1, len(prev.lags))):
+                for d in prev.late_order:
                     pl.when(i < prev.lags[d])(lambda d=d: stage(prev, d, i - prev.lags[d] + G))
-            for d, lag in enumerate(cur.lags):
+            for d in cur.order:
+                lag = cur.lags[d]
                 pl.when(i >= lag + gap)(lambda d=d, lag=lag: stage(cur, d, i - lag - gap))
 
     def finish_last(prev):
         @pl.loop(0, prev.lags[-1])
         def _(i):
-            for d in reversed(range(1, len(prev.lags))):
+            for d in prev.late_order:
                 pl.when(i < prev.lags[d])(lambda d=d: stage(prev, d, i - prev.lags[d] + G))
 
     def wait_all(copies):

time: 114 us -> 114 us (level)
  no operation moved by 1% of the time
where the time goes in v4:
time: 114 us; the launch traced here: 112 us
  Pallas kernels  111 us (97%)
    pallas_call x1, Pallas kernels, per_device(): pl.pallas_call(kernel, out_shape=(jax.ShapeDtypeStruct((STREAMS, SROWS, B...  109 us
    pallas_call x1, Pallas kernels, per_device(): pl.pallas_call(turn, out_shape=(jax.ShapeDtypeStruct((BLK, STEPS, TOK), B...  2.44 us

profile of v4, /device:TPU:24, one launch (start us, length us, event | category | flops | bytes accessed | tf_op | source)
XLA Modules:
  0.0 111.8 jit_solution(9291734047834465557)
XLA Ops:
  0.6 108.7 %layer.1 = (bf16[2,256,128]{2,1,0:T(8,128)(2,1)}, bf16[2,256,128]{2,1,0:T(8,128)(2,1)}) custom-call(bf16[128,4,128]{2,1,0:T(4,128)(2,1)} %bitcast.10, bf16[128,4,128]{2,1,0:T(4,128)(2,1)} %bitcast.11, s32[1,512]{1,0:T(1,128)} %hth_ref.1, s32[1,512]{1,0:T(1,128)} %hwd_ref.1, s32[1,128]{1,0:T(1,128)} %oth_ref.1, s32[1,128]{1,0:T(1,128)} %owd_ref.1, ...), custom_call_target="tpu_custom_call" | custom-call | flops 12884901888 | bytes 12582912 | tf_op jit(solution)/shard_map/layer/pallas_call | solution.py:449
  109.3 2.4 %turn.1 = (bf16[128,4,128]{2,1,0:T(4,128)(2,1)}, bf16[128,4,128]{2,1,0:T(4,128)(2,1)}) custom-call(bf16[2,256,128]{2,1,0:T(8,128)(2,1)} %get-tuple-element.6.inc_rows, bf16[2,256,128]{2,1,0:T(8,128)(2,1)} %get-tuple-element.7.ret_rows), custom_call_target="tpu_custom_call" | custom-call | tf_op jit(solution)/shard_map/turn/pallas_call | solution.py:507

commit v5 on v4

--- a/solution.py
+++ b/solution.py
@@ -108,8 +108,8 @@
 
     class Gather:
         lags = (0, 2, 4, 5)
-        order = (1, 2, 0, 3)
-        late_order = (1, 2, 3)
+        order = (0, 1, 2, 3)
+        late_order = (3, 2, 1)
 
         def __init__(self, n, buf, compute, finish):
             self.n, self.buf, self.compute, self.finish = n, buf, compute, finish

time: 114 us -> 112 us (0.982); the launches traced: 112 us -> 111 us
  no operation moved by 1% of the time
where the time goes in v5:
time: 112 us; the launch traced here: 111 us
  Pallas kernels  111 us (99%)
    pallas_call x1, Pallas kernels, per_device(): pl.pallas_call(kernel, out_shape=(jax.ShapeDtypeStruct((STREAMS, SROWS, B...  108 us
    pallas_call x1, Pallas kernels, per_device(): pl.pallas_call(turn, out_shape=(jax.ShapeDtypeStruct((BLK, STEPS, TOK), B...  2.44 us

profile of v5, /device:TPU:24, one launch (start us, length us, event | category | flops | bytes accessed | tf_op | source)
XLA Modules:
  0.0 111.4 jit_solution(8847801350315744983)
XLA Ops:
  0.6 108.3 %layer.1 = (bf16[2,256,128]{2,1,0:T(8,128)(2,1)}, bf16[2,256,128]{2,1,0:T(8,128)(2,1)}) custom-call(bf16[128,4,128]{2,1,0:T(4,128)(2,1)} %bitcast.10, bf16[128,4,128]{2,1,0:T(4,128)(2,1)} %bitcast.11, s32[1,512]{1,0:T(1,128)} %hth_ref.1, s32[1,512]{1,0:T(1,128)} %hwd_ref.1, s32[1,128]{1,0:T(1,128)} %oth_ref.1, s32[1,128]{1,0:T(1,128)} %owd_ref.1, ...), custom_call_target="tpu_custom_call" | custom-call | flops 12884901888 | bytes 12582912 | tf_op jit(solution)/shard_map/layer/pallas_call | solution.py:449
  108.9 2.4 %turn.1 = (bf16[128,4,128]{2,1,0:T(4,128)(2,1)}, bf16[128,4,128]{2,1,0:T(4,128)(2,1)}) custom-call(bf16[2,256,128]{2,1,0:T(8,128)(2,1)} %get-tuple-element.6.inc_rows, bf16[2,256,128]{2,1,0:T(8,128)(2,1)} %get-tuple-element.7.ret_rows), custom_call_target="tpu_custom_call" | custom-call | tf_op jit(solution)/shard_map/turn/pallas_call | solution.py:507
